TPU v7x, 512 devices: a whole 4x8x8 slice. The times are simulated.
512 devices in a mesh: req: 32 (over y, x), exp: 16 (over z, core).
Axes of the slice: x: 4, y: 8, z: 8, core: 2. Of those that a mesh axis runs over, the one named last changes fastest.
Arguments:
- resid_in: bfloat16 [4096, 3584], P(('req', 'exp')), may hold values from -6 to 6
- queries: bfloat16 [4096, 3584], P(('req', 'exp')), may hold values from -40 to 40
- fresh_kv: bfloat16 [4096, 1024], P(('req', 'exp')), may hold values from -6 to 6
- kv_pool: bfloat16 [32, 16, 32, 16, 1024], P('req', 'exp'), may hold values from -6 to 6
- block_table: int32 [2048, 8], P(('req', 'exp')), may hold values from 0 to 31, as said below
- lengths: int32 [2048], P(('req', 'exp')), may hold values from 1 to 128, as said below
- mig_source: int32 [32, 16, 2, 4], P('req', 'exp'), may hold values from 0 to 31, as said below
- mig_target: int32 [32, 16, 2, 4], P('req', 'exp'), may hold values from 0 to 31, as said below
- expert_ids: int32 [4096, 8], P('req'), may hold values from 0 to 63, all different within a row; in each aligned block of 128 rows (0 to 127, 128 to 255, ...) at most 24 rows name the same one
- gate_values: float32 [4096, 8], P('req'), may hold values from 0.2 to 1
- norm_gain: bfloat16 [3584], replicated, may hold values from 0.5 to 1.5
- w_in: bfloat16 [16, 32, 3584, 256], P('exp', 'req'), may hold values from -0.09375 to 0.09375
- w_out: bfloat16 [16, 32, 256, 3584], P('exp', 'req'), may hold values from -0.125 to 0.125
Outputs:
- mixed: bfloat16 [4096, 3584], P(('req', 'exp'))
Inputs may be any that keep to these rules, and one draw needn't show every extreme that they name: `block_table`: the entries of the 4 rows of one device are distinct pages of that device's pool. `lengths`: A request that arrives by migration has more than (3) * 16 cached positions. `mig_target`: on every device exactly one request arrives from req index - 1 and one from index + 1 (around the loop); [r, e, 0, i] is the page that takes page i of the request from index - 1, [r, e, 1, i] of the one from index + 1; they are the first 4 entries of that request's block-table row. `mig_source`: [r, e, 0, i] is the pool page sent as page i to index + 1, [r, e, 1, i] to index - 1; the 8 pages of a device are distinct and belong to no request that stays on it. `expert_ids`: each row names 8 different experts; among the 128 tokens of one index of req no expert is named by more than 24 rows.
All inputs are finite; a program needn't handle non-finite values.
Results may differ from a plain program's by a relative error of at most 0.012.
Values may be sent and summed in bfloat16 or wider, within the bound.
A program may use at most 64 MiB of HBM per device.

v0:
```python
import jax
import jax.numpy as jnp
from jax import lax
from jax.sharding import PartitionSpec as P

HEADS = 28
KV_HEADS = 4
HEAD_DIM = 128
EXP_DEV = 4
CAP = 24


neg_big = -1e30
norm_eps = 1e-06


def with_halo(block, sides, width):
    for axis, dim in sides:
        count = lax.axis_size(axis)
        forward = [(i, i + 1) for i in range(count - 1)]
        forward.append((count - 1, 0))
        backward = [(target, source) for source, target in forward]
        low = lax.ppermute(
            lax.slice_in_dim(block, block.shape[dim] - width, None, axis=dim), axis, forward
        )
        high = lax.ppermute(lax.slice_in_dim(block, 0, width, axis=dim), axis, backward)
        block = jnp.concatenate([low, block, high], axis=dim)
    return block


def partial_attention(query_grid, key_rows, visible):
    request_count = key_rows.shape[0]
    span = key_rows.shape[1]
    key_width = KV_HEADS * HEAD_DIM
    key_part = key_rows[:, :, :key_width].reshape(request_count, span, KV_HEADS, HEAD_DIM)
    value_part = (
        key_rows[:, :, key_width:]
        .reshape(request_count, span, KV_HEADS, HEAD_DIM)
        .astype(jnp.float32)
    )
    scores = jnp.einsum(
        "rdkgh,rpkh->rdkgp", query_grid, key_part, preferred_element_type=jnp.float32
    ) * HEAD_DIM ** (-0.5)
    live = visible[:, :, None, None, :]
    scores = jnp.where(live, scores, neg_big)
    highest = jnp.max(scores, axis=-1)
    weights = jnp.where(live, jnp.exp(scores - highest[..., None]), 0.0)
    weight_sum = jnp.sum(weights, axis=-1)
    summed = jnp.einsum("rdkgp,rpkh->rdkgh", weights, value_part, precision=lax.Precision.HIGHEST)
    return (highest, weight_sum, summed)


def body(
    resid_in,
    queries,
    fresh_kv,
    kv_pool,
    block_table,
    lengths,
    mig_source,
    mig_target,
    expert_ids,
    gate_values,
    norm_gain,
    w_in,
    w_out,
):
    request_count = block_table.shape[0]
    table_width = block_table.shape[1]
    page_tokens = kv_pool.shape[3]
    kv_width = kv_pool.shape[4]
    cache_span = table_width * page_tokens
    token_count = resid_in.shape[0]
    draft_count = token_count // request_count
    model_width = resid_in.shape[1]
    moved = mig_source.shape[3]
    pool_pages = kv_pool[0, 0]
    sources = mig_source[0, 0]
    target_pairs = mig_target[0, 0]
    outgoing = jnp.concatenate([pool_pages[sources[1]], pool_pages[sources[0]]], axis=0)
    targets = jnp.concatenate([target_pairs[0], target_pairs[1]], axis=0)
    extended = with_halo(outgoing, (("req", 0),), moved)
    arrivals = jnp.concatenate([extended[:moved], extended[-moved:]], axis=0)
    query_grid = queries.reshape(request_count, draft_count, KV_HEADS, HEADS // KV_HEADS, HEAD_DIM)
    fresh_rows = fresh_kv.reshape(request_count, draft_count, kv_width)
    position = jnp.arange(cache_span)
    cache_visible = jnp.broadcast_to(
        position[None, None, :] < lengths[:, None, None], (request_count, draft_count, cache_span)
    )
    draft_index = jnp.arange(draft_count)
    draft_visible = jnp.broadcast_to(
        draft_index[None, :] <= draft_index[:, None], (request_count, draft_count, draft_count)
    )
    pool_after = pool_pages.at[targets].set(arrivals)
    cache_rows = pool_after[block_table].reshape(request_count, cache_span, kv_width)
    parts = partial_attention(
        query_grid,
        jnp.concatenate([cache_rows, fresh_rows], axis=1),
        jnp.concatenate([cache_visible, draft_visible], axis=2),
    )
    attention = (parts[2] / parts[1][..., None]).reshape(token_count, model_width)
    residual = resid_in.astype(jnp.float32) + attention
    inv_rms = lax.rsqrt(jnp.mean(residual * residual, axis=1, keepdims=True) + norm_eps)
    normed = (residual * inv_rms * norm_gain.astype(jnp.float32)).astype(jnp.bfloat16)
    local_ids = lax.axis_index("exp") * EXP_DEV + jnp.arange(EXP_DEV)
    matches = expert_ids[None, :, :] == local_ids[:, None, None]
    is_named = jnp.any(matches, axis=2)
    gate_local = jnp.sum(jnp.where(matches, gate_values[None, :, :], 0.0), axis=2)
    slot_index = jnp.cumsum(is_named.astype(jnp.int32), axis=1) - 1
    placement = is_named[:, None, :] & (slot_index[:, None, :] == jnp.arange(CAP)[None, :, None])
    slot_gate = jnp.sum(jnp.where(placement, gate_local[:, None, :], 0.0), axis=2)
    slot_select = placement.astype(jnp.bfloat16)
    columns = slot_select
    packed = jnp.einsum(
        "kct,td->kcd",
        columns,
        lax.all_gather(normed, "exp", axis=0, tiled=True),
        preferred_element_type=jnp.float32,
    )
    packed = packed.astype(jnp.bfloat16)
    group_size = lax.axis_size("req") // EXP_DEV
    outbound = jnp.repeat(packed, group_size, axis=0)
    inner_weights = w_in[0, 0]
    outer_weights = w_out[0, 0]
    inbound = lax.all_to_all(outbound, "req", split_axis=0, concat_axis=0, tiled=True)
    hidden = jnp.einsum("scd,df->scf", inbound, inner_weights, preferred_element_type=jnp.float32)
    activated = jax.nn.silu(hidden).astype(jnp.bfloat16)
    returned = lax.all_to_all(
        jnp.einsum(
            "scf,fd->scd", activated, outer_weights, preferred_element_type=jnp.float32
        ).astype(jnp.bfloat16),
        "req",
        split_axis=0,
        concat_axis=0,
        tiled=True,
    )
    expert_out = jnp.sum(
        returned.reshape(EXP_DEV, group_size, CAP, model_width).astype(jnp.float32), axis=1
    )
    weighted = expert_out * slot_gate[:, :, None]
    slot_select_wide = placement.astype(jnp.float32)
    columns = slot_select_wide
    expert_mix = lax.psum_scatter(
        jnp.einsum("kct,kcd->td", columns, weighted, precision=lax.Precision.HIGHEST).astype(
            jnp.bfloat16
        ),
        "exp",
        scatter_dimension=0,
        tiled=True,
    ).astype(jnp.float32)
    return (residual + expert_mix).astype(jnp.bfloat16)


def solution(mesh):
    placed = (
        P(("req", "exp"), None),
        P(("req", "exp"), None),
        P(("req", "exp"), None),
        P("req", "exp", None, None, None),
        P(("req", "exp"), None),
        P(("req", "exp")),
        P("req", "exp", None, None),
        P("req", "exp", None, None),
        P("req", None),
        P("req", None),
        P(),
        P("exp", "req", None, None),
        P("exp", "req", None, None),
    )
    return jax.shard_map(
        body, mesh=mesh, in_specs=placed, out_specs=P(("req", "exp"), None), check_vma=False
    )
```

profile of v0, /device:TPU:1, one launch (start us, length us, event | category | flops | bytes accessed | tf_op | source)
XLA Modules:
  0.0 399.6 jit_solution(36043764672212285)
XLA Ops:
  6.6 1.4 copy.45
  8.0 0.6 gather_fusion
  8.5 3.9 collective-permute-start
  12.5 0.6 gather_fusion.1
  13.0 6.1 %collective-permute-start.1 = (bf16[4,16,1024]{2,1,0:T(8,128)(2,1)S(1)}, bf16[4,16,1024]{2,1,0:T(8,128)(2,1)S(1)}, u32[]{:S(2)}, u32[]{:S(2)}) collective-permute-start(bf16[4,16,1024]{2,1,0:T(8,128)(2,1)S(1)} %gather_fusion.1), channel_id=1, source_target_pairs={{16,0},{32,16},{48,32},{64,48},{80,64},{96,80},{112,96},{128,112},... | collective-permute-start | bytes 393224 | tf_op jit(solution)/shard_map/ppermute | solution.py:26
  19.3 0.6 pad_clamp_fusion
  19.9 0.7 iota_compare_fusion.1
  21.5 0.6 fusion.31
  22.2 1.3 convert_element_type.45
  23.6 0.7 broadcast_in_dim.77
  24.3 0.9 scatter_fusion
  25.2 1.7 gather_fusion.2
  26.9 1.3 pad_maximum_fusion
  28.6 0.5 fusion.36
  29.4 0.6 fusion.7
  30.3 26.5 %all_gather.3 = bf16[128,3584]{1,0:T(8,128)(2,1)S(1)} all-gather(bf16[8,3584]{1,0:T(8,128)(2,1)S(1)} %multiply_convert_fusion.1), channel_id=1, replica_groups=mesh['req'=32,'exp'=16] {'exp'}, dimensions={0}, use_global_device_ids=true | all-gather | bytes 974848 | tf_op jit(solution)/shard_map/all_gather | solution.py:117
  57.5 131.9 %all_to_all.10 = bf16[32,24,3584]{2,1,0:T(8,128)(2,1)} all-to-all(bf16[32,24,3584]{2,1,0:T(8,128)(2,1)S(1)} %bitcast.52), channel_id=1, replica_groups=mesh['req'=32,'exp'=16] {'req'}, dimensions={0} | all-to-all | bytes 11010048 | tf_op jit(solution)/shard_map/all_to_all | solution.py:125
  189.4 11.5 %convolution_convert_fusion = bf16[32,24,3584]{2,1,0:T(8,128)(2,1)} fusion(bf16[1,1,256,3584]{3,2,1,0:T(8,128)(2,1)S(1)} %copy-done, bf16[32,24,3584]{2,1,0:T(8,128)(2,1)} %all_to_all.10, bf16[1,1,3584,256]{3,2,1,0:T(8,128)(2,1)} %param.24), kind=kOutput, calls=%fused_computation.5 | convolution fusion | flops 2822307840 | bytes 14680064 | tf_op jit(solution)/shard_map/scf,fd->scd/dot_general | solution.py:129
  201.0 5.0 %all-to-all-start.1 = ((bf16[32,24,3584]{2,1,0:T(8,128)(2,1)}), bf16[32,24,3584]{2,1,0:T(8,128)(2,1)}, u32[]{:S(2)}, u32[]{:S(2)}) async-start(bf16[32,24,3584]{2,1,0:T(8,128)(2,1)} %convolution_convert_fusion), calls=%async_computation.1 | async-start | bytes 11010048 | tf_op jit(solution)/shard_map/all_to_all | solution.py:128
  206.3 119.6 %all-to-all-done.1 = bf16[32,24,3584]{2,1,0:T(8,128)(2,1)} async-done(((bf16[32,24,3584]{2,1,0:T(8,128)(2,1)}), bf16[32,24,3584]{2,1,0:T(8,128)(2,1)}, u32[]{:S(2)}, u32[]{:S(2)}) %all-to-all-start.1) | async-done | bytes 5505056 | tf_op jit(solution)/shard_map/all_to_all | solution.py:128
  325.9 3.5 convert_reduce_fusion
  329.3 2.0 fusion
  331.3 60.0 %reduce-scatter.2.cloned.1.call-done = bf16[8,3584]{1,0:T(8,128)(2,1)} async-done(((bf16[128,3584]{1,0:T(8,128)(2,1)}), bf16[8,3584]{1,0:T(8,128)(2,1)}) %reduce-scatter.2.cloned.1.call-update) | async-done | bytes 57360 | tf_op jit(solution)/shard_map/reduce_scatter | solution.py:143
  391.3 1.5 add_convert_fusion
  (65 shorter events, 3.1 us)
Async XLA Ops:
  6.5 182.9 %copy-start = (bf16[1,1,256,3584]{3,2,1,0:T(8,128)(2,1)S(1)}, bf16[1,1,256,3584]{3,2,1,0:T(8,128)(2,1)}, u32[]{:S(2)}) copy-start(bf16[1,1,256,3584]{3,2,1,0:T(8,128)(2,1)} %param.25) | copy-start | bytes 5505028
  6.5 15.6 %copy-start.3 = (bf16[8,3584]{1,0:T(8,128)(2,1)S(1)}, bf16[8,3584]{1,0:T(8,128)(2,1)}, u32[]{:S(2)}) copy-start(bf16[8,3584]{1,0:T(8,128)(2,1)} %param.14) | copy-start | bytes 172036
  6.5 15.6 %copy-start.6 = (bf16[8,1024]{1,0:T(8,128)(2,1)S(1)}, bf16[8,1024]{1,0:T(8,128)(2,1)}, u32[]{:S(2)}) copy-start(bf16[8,1024]{1,0:T(8,128)(2,1)} %param.15) | copy-start | bytes 49156
  6.5 12.6 %copy-start.10 = (s32[4,8]{1,0:T(4,128)S(1)}, s32[4,8]{1,0:T(4,128)}, u32[]{:S(2)}) copy-start(s32[4,8]{1,0:T(4,128)} %param.17) | copy-start | bytes 388
  6.5 13.3 %copy-start.15 = (s32[4]{0:T(128)S(1)}, s32[4]{0:T(128)}, u32[]{:S(2)}) copy-start(s32[4]{0:T(128)} %param.18) | copy-start | bytes 52
  6.5 1.4 copy-start.13
  6.6 12.6 %copy-start.14 = (s32[1,1,2,4]{3,2,1,0:T(2,128)S(1)}, s32[1,1,2,4]{3,2,1,0:T(2,128)}, u32[]{:S(2)}) copy-start(s32[1,1,2,4]{3,2,1,0:T(2,128)} %param.20) | copy-start | bytes 100
  6.6 14.0 %copy-start.4 = (s32[128,8]{0,1:T(8,128)S(1)}, s32[128,8]{0,1:T(8,128)}, u32[]{:S(2)}) copy-start(s32[128,8]{0,1:T(8,128)} %param.21) | copy-start | bytes 12292
  8.5 15.7 %collective-permute-start = (bf16[4,16,1024]{2,1,0:T(8,128)(2,1)S(1)}, bf16[4,16,1024]{2,1,0:T(8,128)(2,1)S(1)}, u32[]{:S(2)}, u32[]{:S(2)}) collective-permute-start(bf16[4,16,1024]{2,1,0:T(8,128)(2,1)S(1)} %gather_fusion), channel_id=1, source_target_pairs={{0,16},{16,32},{32,48},{48,64},{64,80},{80,96},{96,112},{112,128},... | collective-permute-start | bytes 393224 | tf_op jit(solution)/shard_map/ppermute | solution.py:23
  13.0 11.2 %collective-permute-start.1 = (bf16[4,16,1024]{2,1,0:T(8,128)(2,1)S(1)}, bf16[4,16,1024]{2,1,0:T(8,128)(2,1)S(1)}, u32[]{:S(2)}, u32[]{:S(2)}) collective-permute-start(bf16[4,16,1024]{2,1,0:T(8,128)(2,1)S(1)} %gather_fusion.1), channel_id=1, source_target_pairs={{16,0},{32,16},{48,32},{64,48},{80,64},{96,80},{112,96},{128,112},... | collective-permute-start | bytes 393224 | tf_op jit(solution)/shard_map/ppermute | solution.py:26
  20.5 0.5 copy-start.11
  21.0 0.5 copy-start.7
  28.6 1.4 copy-start.1
  28.6 1.6 copy-start.2
  29.3 27.4 %copy-start.8 = (pred[4,128]{1,0:T(4,128)(4,1)S(1)}, pred[4,128]{1,0:T(4,128)(4,1)}, u32[]{:S(2)}) copy-start(pred[4,128]{1,0:T(4,128)(4,1)} %copy-done.7) | copy-start | bytes 1540
  201.0 5.1 %copy-start.5 = (s32[128,8]{0,1:T(8,128)S(1)}, s32[128,8]{0,1:T(8,128)}, u32[]{:S(2)}) copy-start(s32[128,8]{0,1:T(8,128)} %param.21) | copy-start | bytes 12292
  201.0 5.1 %copy-start.9 = (f32[128,8]{0,1:T(8,128)S(1)}, f32[128,8]{0,1:T(8,128)}, u32[]{:S(2)}) copy-start(f32[128,8]{0,1:T(8,128)} %param.22) | copy-start | bytes 12292
  201.0 5.1 %copy-start.12 = (s32[4]{0:T(128)S(1)}, s32[4]{0:T(128)}, u32[]{:S(2)}) copy-start(s32[4]{0:T(128)} %copy-done.11) | copy-start | bytes 52
  201.0 124.9 %all-to-all-start.1 = ((bf16[32,24,3584]{2,1,0:T(8,128)(2,1)}), bf16[32,24,3584]{2,1,0:T(8,128)(2,1)}, u32[]{:S(2)}, u32[]{:S(2)}) async-start(bf16[32,24,3584]{2,1,0:T(8,128)(2,1)} %convolution_convert_fusion), calls=%async_computation.1 | async-start | bytes 11010048 | tf_op jit(solution)/shard_map/all_to_all | solution.py:128
  206.0 185.2 %reduce-scatter.2.cloned.1.call-start = ((), (), s32[]{:S(2)}) async-start(), calls=%async_computation.3 | async-start | bytes 974848 | tf_op jit(solution)/shard_map/reduce_scatter | solution.py:143
Sparse Core Ops, SparseCore 0:
  331.4 59.7 reduce-scatter.1
where the time goes:
time: 402 us; the launch traced here: 400 us
  waiting for transfers between devices  180 us (45%)
  blocking collectives  158 us (39%)
  starting transfers between devices  15.1 us (4%)
  matrix products  14.9 us (4%)
  between operations  13.7 us (3%)
  other arithmetic  10.5 us (3%)
  local copies, waits for them, and re-layouts  7.34 us (2%)
    all_to_all x1, blocking collectives, body(): lax.all_to_all(outbound, 'req', split_axis=0, concat_axis=0, tiled=True)  132 us
    all_to_all x1, waiting for transfers between devices, body(): lax.all_to_all(jnp.einsum('scf,fd->scd', activated, outer_weights, prefer...  120 us
    reduce_scatter x1, waiting for transfers between devices, body(): lax.psum_scatter(jnp.einsum('kct,kcd->td', columns, weighted, precision=l...  60 us
    all_gather x1, blocking collectives, body(): lax.all_gather(normed, 'exp', axis=0, tiled=True)  26.5 us
    dot_general x1, matrix products, body(): jnp.einsum('scf,fd->scd', activated, outer_weights, preferred_element_typ...  11.5 us
  transfers between devices with their start and end apart: 4, of which 2 were waited for; matrix products, arithmetic and copies ran while one was open for 1% of the time, Pallas kernels for 0%

commit v1 on v0

--- a/solution.py
+++ b/solution.py
@@ -1,6 +1,10 @@
+import functools
+
 import jax
 import jax.numpy as jnp
 from jax import lax
+from jax.experimental import pallas as pl
+from jax.experimental.pallas import tpu as pltpu
 from jax.sharding import PartitionSpec as P
 
 HEADS = 28
@@ -8,10 +12,13 @@
 HEAD_DIM = 128
 EXP_DEV = 4
 CAP = 24
-
+NX = 4
+NY = 8
+CHUNKS = 7
 
 neg_big = -1e30
 norm_eps = 1e-06
+MESH = pl.DeviceIdType.MESH
 
 
 def with_halo(block, sides, width):
@@ -48,6 +55,300 @@
     weight_sum = jnp.sum(weights, axis=-1)
     summed = jnp.einsum("rdkgp,rpkh->rdkgh", weights, value_part, precision=lax.Precision.HIGHEST)
     return (highest, weight_sum, summed)
+
+
+def wait_bytes(ref, sem):
+    pltpu.make_async_copy(ref, ref, sem).wait()
+
+
+def moe_kernel(
+    packed,
+    mix_hi,
+    mix_lo,
+    w_in,
+    w_out,
+    out,
+    grid_in,
+    part,
+    relay_in,
+    direct_in,
+    summed,
+    back,
+    w1,
+    w2,
+    hidden,
+    act,
+    load_sem,
+    own_sem,
+    y_send,
+    y_recv,
+    x_send,
+    x_recv,
+    r_send,
+    r_recv,
+    br_send,
+    br_recv,
+    bd_send,
+    bd_recv,
+    by_own,
+    by_send,
+    by_recv,
+):
+    me = lax.axis_index("req")
+    ex = lax.axis_index("exp")
+    x = lax.rem(me, NX)
+    y = lax.div(me, NX)
+    width = w1.shape[0] // CHUNKS
+    row = y * NX
+    xp = lax.rem(x + 1, NX)
+    xm = lax.rem(x + NX - 1, NX)
+    xo = lax.rem(x + 2, NX)
+    right = (row + xp, ex)
+    left = (row + xm, ex)
+
+    def ydev(j):
+        yd = lax.rem(y + j, NY)
+        return yd, (yd * NX + x, ex)
+
+    barrier = pltpu.get_barrier_semaphore()
+    for peer in (left, right):
+        pl.semaphore_signal(barrier, inc=1, device_id=peer, device_id_type=MESH)
+    for j in range(1, NY):
+        pl.semaphore_signal(barrier, inc=1, device_id=ydev(j)[1], device_id_type=MESH)
+    load1 = pltpu.make_async_copy(w_in, w1, load_sem.at[0])
+    load2 = pltpu.make_async_copy(w_out, w2, load_sem.at[1])
+    load1.start()
+    load2.start()
+    hidden[...] = jnp.zeros_like(hidden)
+    pl.semaphore_wait(barrier, 2 + NY - 1)
+
+    def span(i):
+        return pl.ds(pl.multiple_of(i * width, 128), width)
+
+    def remote(src, dst, send, recv, dev):
+        return pltpu.make_async_remote_copy(
+            src_ref=src, dst_ref=dst, send_sem=send, recv_sem=recv, device_id=dev, device_id_type=MESH
+        )
+
+    def issue_y(i, c):
+        cols = span(i)
+        pltpu.make_async_copy(
+            packed.at[lax.div(y, 2), :, cols], grid_in.at[x, y, :, cols], own_sem.at[i]
+        ).start()
+        for j in range(1, NY):
+            yd, dev = ydev(j)
+            remote(
+                packed.at[lax.div(yd, 2), :, cols],
+                grid_in.at[x, y, :, cols],
+                y_send.at[i],
+                y_recv.at[i],
+                dev,
+            ).start()
+        return c
+
+    lax.fori_loop(0, CHUNKS, issue_y, 0)
+    load1.wait()
+    low, high = pl.ds(0, NY // 2), pl.ds(NY // 2, NY // 2)
+
+    def seven(i):
+        return grid_in.at[0, pl.ds(0, NY - 1), :, span(i)]
+
+    def inward(i, c):
+        @pl.when(i < CHUNKS)
+        def _():
+            cols = span(i)
+            wait_bytes(grid_in.at[0, 0, :, cols], own_sem.at[i])
+            wait_bytes(seven(i), y_recv.at[i])
+            block = grid_in.at[x, :, :, cols]
+            remote(block, block, x_send.at[i, 0], x_recv.at[i, 0], right).start()
+            remote(block, block, x_send.at[i, 1], x_recv.at[i, 1], left).start()
+
+        @pl.when((i >= 1) & (i < CHUNKS + 1))
+        def _():
+            n = i - 1
+            cols = span(n)
+            wait_bytes(grid_in.at[xm, :, :, cols], x_recv.at[n, 0])
+            block = grid_in.at[xm, low, :, cols]
+            remote(block, block, r_send.at[n, 0], r_recv.at[n, 0], right).start()
+            wait_bytes(grid_in.at[xp, :, :, cols], x_recv.at[n, 1])
+            block = grid_in.at[xp, high, :, cols]
+            remote(block, block, r_send.at[n, 1], r_recv.at[n, 1], left).start()
+
+        @pl.when(i >= 2)
+        def _():
+            n = i - 2
+            cols = span(n)
+            wait_bytes(grid_in.at[xo, low, :, cols], r_recv.at[n, 0])
+            wait_bytes(grid_in.at[xo, high, :, cols], r_recv.at[n, 1])
+            weight = w1[span(n), :]
+            for b in range(NX):
+                hidden[b] += jnp.dot(
+                    grid_in[b, :, :, cols].reshape(NY * CAP, width),
+                    weight,
+                    preferred_element_type=jnp.float32,
+                )
+
+        return c
+
+    lax.fori_loop(0, CHUNKS + 2, inward, 0)
+    for b in range(NX):
+        v = hidden[b]
+        act[b] = (v / (1.0 + jnp.exp(-v))).astype(jnp.bfloat16)
+    load2.wait()
+
+    def outward(i, c):
+        @pl.when(i < CHUNKS)
+        def _():
+            cols = span(i)
+
+            def product(b):
+                part[b, :, :, cols] = (
+                    jnp.dot(act[b], w2[:, cols], preferred_element_type=jnp.float32)
+                    .astype(jnp.bfloat16)
+                    .reshape(NY, CAP, width)
+                )
+
+            product(xo)
+            product(xm)
+            product(xp)
+            remote(
+                part.at[xo, low, :, cols], relay_in.at[0, :, :, cols],
+                br_send.at[i, 0], br_recv.at[i, 0], left,
+            ).start()
+            remote(
+                part.at[xo, high, :, cols], relay_in.at[1, :, :, cols],
+                br_send.at[i, 1], br_recv.at[i, 1], right,
+            ).start()
+            product(x)
+            remote(
+                part.at[xm, high, :, cols], direct_in.at[0, high, :, cols],
+                bd_send.at[i, 0], bd_recv.at[i, 0], left,
+            ).start()
+            remote(
+                part.at[xp, low, :, cols], direct_in.at[1, low, :, cols],
+                bd_send.at[i, 1], bd_recv.at[i, 1], right,
+            ).start()
+
+        @pl.when((i >= 1) & (i < CHUNKS + 1))
+        def _():
+            n = i - 1
+            cols = span(n)
+
+            def added(b, rows, side):
+                wait_bytes(relay_in.at[side, :, :, cols], br_recv.at[n, side])
+                part[b, rows, :, cols] = (
+                    part[b, rows, :, cols].astype(jnp.float32)
+                    + relay_in[side, :, :, cols].astype(jnp.float32)
+                ).astype(jnp.bfloat16)
+
+            added(xm, low, 0)
+            added(xp, high, 1)
+            remote(
+                part.at[xm, low, :, cols], direct_in.at[0, low, :, cols],
+                bd_send.at[n, 2], bd_recv.at[n, 2], left,
+            ).start()
+            remote(
+                part.at[xp, high, :, cols], direct_in.at[1, high, :, cols],
+                bd_send.at[n, 3], bd_recv.at[n, 3], right,
+            ).start()
+
+        @pl.when((i >= 2) & (i < CHUNKS + 2))
+        def _():
+            n = i - 2
+            cols = span(n)
+            wait_bytes(direct_in.at[0, high, :, cols], bd_recv.at[n, 0])
+            wait_bytes(direct_in.at[1, low, :, cols], bd_recv.at[n, 1])
+            wait_bytes(direct_in.at[0, low, :, cols], bd_recv.at[n, 2])
+            wait_bytes(direct_in.at[1, high, :, cols], bd_recv.at[n, 3])
+            summed[:, :, cols] = (
+                part[x, :, :, cols].astype(jnp.float32)
+                + direct_in[0, :, :, cols].astype(jnp.float32)
+                + direct_in[1, :, :, cols].astype(jnp.float32)
+            ).astype(jnp.bfloat16)
+            pltpu.make_async_copy(
+                summed.at[y, :, cols], back.at[y, :, cols], by_own.at[n]
+            ).start()
+            for j in range(1, NY):
+                yd, dev = ydev(j)
+                remote(
+                    summed.at[yd, :, cols], back.at[y, :, cols], by_send.at[n], by_recv.at[n], dev
+                ).start()
+
+        @pl.when(i >= 3)
+        def _():
+            n = i - 3
+            cols = span(n)
+            wait_bytes(back.at[0, :, cols], by_own.at[n])
+            wait_bytes(back.at[pl.ds(0, NY - 1), :, cols], by_recv.at[n])
+            rows = back[:, :, cols].reshape(NY * CAP, width)
+            out[:, cols] = (
+                jnp.dot(mix_hi[...], rows, preferred_element_type=jnp.float32)
+                + jnp.dot(mix_lo[...], rows, preferred_element_type=jnp.float32)
+            ).astype(jnp.bfloat16)
+
+        return c
+
+    lax.fori_loop(0, CHUNKS + 3, outward, 0)
+
+    def drain(i, c):
+        cols = span(i)
+        half = relay_in.at[0, :, :, cols]
+        wait_bytes(seven(i), y_send.at[i])
+        for s in range(2):
+            wait_bytes(grid_in.at[0, :, :, cols], x_send.at[i, s])
+            wait_bytes(half, r_send.at[i, s])
+            wait_bytes(half, br_send.at[i, s])
+        for s in range(4):
+            wait_bytes(half, bd_send.at[i, s])
+        wait_bytes(back.at[pl.ds(0, NY - 1), :, cols], by_send.at[i])
+        return c
+
+    lax.fori_loop(0, CHUNKS, drain, 0)
+
+
+def moe(packed, mix_hi, mix_lo, w_in, w_out):
+    depth, units = w_in.shape
+    bf = jnp.bfloat16
+    vmem = pl.BlockSpec(memory_space=pltpu.VMEM)
+    anywhere = pl.BlockSpec(memory_space=pl.ANY)
+    dma = pltpu.SemaphoreType.DMA
+    return pl.pallas_call(
+        moe_kernel,
+        name="moe_plane",
+        out_shape=jax.ShapeDtypeStruct((mix_hi.shape[0], depth), bf),
+        in_specs=[vmem, vmem, vmem, anywhere, anywhere],
+        out_specs=vmem,
+        scratch_shapes=[
+            pltpu.VMEM((NX, NY, CAP, depth), bf),
+            pltpu.VMEM((NX, NY, CAP, depth), bf),
+            pltpu.VMEM((2, NY // 2, CAP, depth), bf),
+            pltpu.VMEM((2, NY, CAP, depth), bf),
+            pltpu.VMEM((NY, CAP, depth), bf),
+            pltpu.VMEM((NY, CAP, depth), bf),
+            pltpu.VMEM((depth, units), bf),
+            pltpu.VMEM((units, depth), bf),
+            pltpu.VMEM((NX, NY * CAP, units), jnp.float32),
+            pltpu.VMEM((NX, NY * CAP, units), bf),
+            dma((2,)),
+            dma((CHUNKS,)),
+            dma((CHUNKS,)),
+            dma((CHUNKS,)),
+            dma((CHUNKS, 2)),
+            dma((CHUNKS, 2)),
+            dma((CHUNKS, 2)),
+            dma((CHUNKS, 2)),
+            dma((CHUNKS, 2)),
+            dma((CHUNKS, 2)),
+            dma((CHUNKS, 4)),
+            dma((CHUNKS, 4)),
+            dma((CHUNKS,)),
+            dma((CHUNKS,)),
+            dma((CHUNKS,)),
+        ],
+        compiler_params=pltpu.CompilerParams(
+            collective_id=0, has_side_effects=True, vmem_limit_bytes=56 * 1024 * 1024
+        ),
+    )(packed, mix_hi, mix_lo, w_in, w_out)
 
 
 def body(
@@ -108,46 +409,22 @@
     gate_local = jnp.sum(jnp.where(matches, gate_values[None, :, :], 0.0), axis=2)
     slot_index = jnp.cumsum(is_named.astype(jnp.int32), axis=1) - 1
     placement = is_named[:, None, :] & (slot_index[:, None, :] == jnp.arange(CAP)[None, :, None])
-    slot_gate = jnp.sum(jnp.where(placement, gate_local[:, None, :], 0.0), axis=2)
     slot_select = placement.astype(jnp.bfloat16)
-    columns = slot_select
     packed = jnp.einsum(
         "kct,td->kcd",
-        columns,
+        slot_select,
         lax.all_gather(normed, "exp", axis=0, tiled=True),
         preferred_element_type=jnp.float32,
-    )
-    packed = packed.astype(jnp.bfloat16)
-    group_size = lax.axis_size("req") // EXP_DEV
-    outbound = jnp.repeat(packed, group_size, axis=0)
-    inner_weights = w_in[0, 0]
-    outer_weights = w_out[0, 0]
-    inbound = lax.all_to_all(outbound, "req", split_axis=0, concat_axis=0, tiled=True)
-    hidden = jnp.einsum("scd,df->scf", inbound, inner_weights, preferred_element_type=jnp.float32)
-    activated = jax.nn.silu(hidden).astype(jnp.bfloat16)
-    returned = lax.all_to_all(
-        jnp.einsum(
-            "scf,fd->scd", activated, outer_weights, preferred_element_type=jnp.float32
-        ).astype(jnp.bfloat16),
-        "req",
-        split_axis=0,
-        concat_axis=0,
-        tiled=True,
-    )
-    expert_out = jnp.sum(
-        returned.reshape(EXP_DEV, group_size, CAP, model_width).astype(jnp.float32), axis=1
-    )
-    weighted = expert_out * slot_gate[:, :, None]
-    slot_select_wide = placement.astype(jnp.float32)
-    columns = slot_select_wide
-    expert_mix = lax.psum_scatter(
-        jnp.einsum("kct,kcd->td", columns, weighted, precision=lax.Precision.HIGHEST).astype(
-            jnp.bfloat16
-        ),
-        "exp",
-        scatter_dimension=0,
-        tiled=True,
-    ).astype(jnp.float32)
+    ).astype(jnp.bfloat16)
+    gated = jnp.where(placement, gate_local[:, None, :], 0.0)
+    gated = jnp.broadcast_to(gated[:, None], (EXP_DEV, NY // EXP_DEV) + gated.shape[1:])
+    mix = gated.reshape(NY * CAP, -1).T
+    mix_hi = lax.reduce_precision(mix, 8, 7)
+    mix_lo = (mix - mix_hi).astype(jnp.bfloat16)
+    mixed_rows = moe(packed, mix_hi.astype(jnp.bfloat16), mix_lo, w_in[0, 0], w_out[0, 0])
+    expert_mix = lax.psum_scatter(mixed_rows, "exp", scatter_dimension=0, tiled=True).astype(
+        jnp.float32
+    )
     return (residual + expert_mix).astype(jnp.bfloat16)
 
 

time: 402 us -> 237 us (0.59)
  blocking collectives: 158 us -> 27.3 us
  waiting for transfers between devices: 180 us -> 58.2 us
  Pallas kernels: 0 us -> 115 us
  matrix products: 14.9 us -> 2.32 us
  other arithmetic: 10.5 us -> 3.44 us
  starting transfers between devices: 15.1 us -> 10.1 us
    all_to_all x1 -> x0, blocking collectives: 132 us -> none  [body(): lax.all_to_all(outbound, 'req', split_axis=0, concat_axis=0, tiled=True)]
    all_to_all x1 -> x0, waiting for transfers between devices: 120 us -> none  [body(): lax.all_to_all(jnp.einsum('scf,fd->scd', activated, outer_weights, prefer...]
    pallas_call x0 -> x1, Pallas kernels: none -> 115 us  [moe(): pl.pallas_call(moe_kernel, name='moe_plane', out_shape=jax.ShapeDtypeStru...]
    dot_general x3 -> x1, matrix products: 13.8 us -> 1.21 us  [body(): jnp.einsum('kct,td->kcd', slot_select, lax.all_gather(normed, 'exp', axis...]
    all_to_all x1 -> x0, starting transfers between devices: 5.03 us -> none  [body(): lax.all_to_all(jnp.einsum('scf,fd->scd', activated, outer_weights, prefer...]
  transfers between devices with their start and end apart: 4 -> 3, of which waited for: 2 -> 2; matrix products, arithmetic and copies ran while one was open for 1% -> 1% of each run, Pallas kernels for 0% -> 0%
where the time goes in v1:
time: 237 us; the launch traced here: 235 us
  Pallas kernels  115 us (49%)
  waiting for transfers between devices  58.2 us (25%)
  blocking collectives  27.3 us (12%)
  between operations  13.7 us (6%)
  starting transfers between devices  10.1 us (4%)
  local copies, waits for them, and re-layouts  4.59 us (2%)
  other arithmetic  3.44 us (1%)
    pallas_call x1, Pallas kernels, moe(): pl.pallas_call(moe_kernel, name='moe_plane', out_shape=jax.ShapeDtypeStru...  115 us
    reduce_scatter x1, waiting for transfers between devices, body(): lax.psum_scatter(mixed_rows, 'exp', scatter_dimension=0, tiled=True)  58.1 us
    all_gather x1, blocking collectives, body(): lax.all_gather(normed, 'exp', axis=0, tiled=True)  27.3 us
    ppermute x1, starting transfers between devices, with_halo(): lax.ppermute(lax.slice_in_dim(block, 0, width, axis=dim), axis, backward)  6.09 us
  transfers between devices with their start and end apart: 3, of which 2 were waited for; matrix products, arithmetic and copies ran while one was open for 1% of the time, Pallas kernels for 0%

profile of v1, /device:TPU:1, one launch (start us, length us, event | category | flops | bytes accessed | tf_op | source)
XLA Modules:
  0.0 234.5 jit_solution(8674678283026497820)
XLA Ops:
  6.6 1.3 copy.49
  7.9 0.6 gather_fusion
  8.5 3.9 %collective-permute-start = (bf16[4,16,1024]{2,1,0:T(8,128)(2,1)S(1)}, bf16[4,16,1024]{2,1,0:T(8,128)(2,1)S(1)}, u32[]{:S(2)}, u32[]{:S(2)}) collective-permute-start(bf16[4,16,1024]{2,1,0:T(8,128)(2,1)S(1)} %gather_fusion), channel_id=1, source_target_pairs={{0,16},{16,32},{32,48},{48,64},{64,80},{80,96},{96,112},{112,128},... | collective-permute-start | bytes 393224 | tf_op jit(solution)/shard_map/ppermute | solution.py:30
  12.4 0.6 gather_fusion.1
  13.0 6.1 %collective-permute-start.1 = (bf16[4,16,1024]{2,1,0:T(8,128)(2,1)S(1)}, bf16[4,16,1024]{2,1,0:T(8,128)(2,1)S(1)}, u32[]{:S(2)}, u32[]{:S(2)}) collective-permute-start(bf16[4,16,1024]{2,1,0:T(8,128)(2,1)S(1)} %gather_fusion.1), channel_id=1, source_target_pairs={{16,0},{32,16},{48,32},{64,48},{80,64},{96,80},{112,96},{128,112},... | collective-permute-start | bytes 393224 | tf_op jit(solution)/shard_map/ppermute | solution.py:33
  19.4 0.3 reduce_window_sum.11
  19.9 0.1 copy.30
  20.0 0.7 fusion.8
  20.9 0.1 collective-permute-done.1
  21.0 0.8 scatter_fusion
  21.8 0.6 gather_fusion.2
  22.4 0.1 pad_maximum_fusion
  22.5 0.2 reshape.228
  22.7 0.2 reshape.227
  22.9 0.5 fusion.23
  23.4 0.2 fusion.7
  23.6 0.6 fusion.2
  24.3 0.1 copy-done
  24.4 0.1 multiply_reduce_fusion
  24.7 27.3 %all_gather.3 = bf16[128,3584]{1,0:T(8,128)(2,1)S(1)} all-gather(bf16[8,3584]{1,0:T(8,128)(2,1)S(1)} %multiply_convert_fusion), channel_id=1, replica_groups=mesh['req'=32,'exp'=16] {'exp'}, dimensions={0}, use_global_device_ids=true | all-gather | bytes 974848 | tf_op jit(solution)/shard_map/all_gather | solution.py:416
  52.0 1.2 convolution_convert_fusion.packed
  53.2 114.9 %moe_plane.1 = bf16[128,3584]{1,0:T(8,128)(2,1)} custom-call(bf16[4,24,3584]{2,1,0:T(8,128)(2,1)} %convolution_convert_fusion.packed, bf16[128,192]{1,0:T(8,128)(2,1)} %get-tuple-element.8.mix_hi, bf16[128,192]{1,0:T(8,128)(2,1)} %get-tuple-element.7.mix_lo, bf16[3584,256]{1,0:T(8,128)(2,1)} %bitcast.39, bf16[256,3584]{1,0:T(8,128)(2,1)} %bitcast.40), custom_call_target="tpu_custom_call" | custom-call | tf_op jit(solution)/shard_map/moe_plane/pallas_call | solution.py:315
  168.1 58.1 %reduce-scatter.2.cloned.1.call-done = bf16[8,3584]{1,0:T(8,128)(2,1)} async-done(((bf16[128,3584]{1,0:T(8,128)(2,1)}), bf16[8,3584]{1,0:T(8,128)(2,1)}) %reduce-scatter.2.cloned.1.call-update) | async-done | bytes 57360 | tf_op jit(solution)/shard_map/reduce_scatter | solution.py:425
  226.2 1.5 add_convert_fusion
  (50 shorter events, 0.9 us)
Async XLA Ops:
  6.5 12.6 %copy-start.6 = (s32[4,8]{1,0:T(4,128)S(1)}, s32[4,8]{1,0:T(4,128)}, u32[]{:S(2)}) copy-start(s32[4,8]{1,0:T(4,128)} %param.17) | copy-start | bytes 388
  6.5 12.7 %copy-start.9 = (s32[4]{0:T(128)S(1)}, s32[4]{0:T(128)}, u32[]{:S(2)}) copy-start(s32[4]{0:T(128)} %param.18) | copy-start | bytes 52
  6.5 1.3 copy-start.7
  6.5 12.6 %copy-start.8 = (s32[1,1,2,4]{3,2,1,0:T(2,128)S(1)}, s32[1,1,2,4]{3,2,1,0:T(2,128)}, u32[]{:S(2)}) copy-start(s32[1,1,2,4]{3,2,1,0:T(2,128)} %param.20) | copy-start | bytes 100
  6.5 12.8 %copy-start.2 = (s32[128,8]{0,1:T(8,128)S(1)}, s32[128,8]{0,1:T(8,128)}, u32[]{:S(2)}) copy-start(s32[128,8]{0,1:T(8,128)} %param.21) | copy-start | bytes 12292
  6.5 13.2 %copy-start.5 = (f32[128,8]{0,1:T(8,128)S(1)}, f32[128,8]{0,1:T(8,128)}, u32[]{:S(2)}) copy-start(f32[128,8]{0,1:T(8,128)} %param.22) | copy-start | bytes 12292
  6.6 219.7 %reduce-scatter.2.cloned.1.call-start = ((), (), s32[]{:S(2)}) async-start(), calls=%async_computation.1 | async-start | bytes 974848 | tf_op jit(solution)/shard_map/reduce_scatter | solution.py:425
  7.9 12.8 %copy-start.3 = (bf16[8,1024]{1,0:T(8,128)(2,1)S(1)}, bf16[8,1024]{1,0:T(8,128)(2,1)}, u32[]{:S(2)}) copy-start(bf16[8,1024]{1,0:T(8,128)(2,1)} %param.15) | copy-start | bytes 49156
  7.9 12.9 %copy-start.1 = (bf16[8,3584]{1,0:T(8,128)(2,1)S(1)}, bf16[8,3584]{1,0:T(8,128)(2,1)}, u32[]{:S(2)}) copy-start(bf16[8,3584]{1,0:T(8,128)(2,1)} %param.14) | copy-start | bytes 172036
  7.9 13.0 %copy-start.4 = (bf16[3584]{0:T(1024)(128)(2,1)S(1)}, bf16[3584]{0:T(1024)(128)(2,1)}, u32[]{:S(2)}) copy-start(bf16[3584]{0:T(1024)(128)(2,1)} %param.23) | copy-start | bytes 21508
  8.5 12.4 %collective-permute-start = (bf16[4,16,1024]{2,1,0:T(8,128)(2,1)S(1)}, bf16[4,16,1024]{2,1,0:T(8,128)(2,1)S(1)}, u32[]{:S(2)}, u32[]{:S(2)}) collective-permute-start(bf16[4,16,1024]{2,1,0:T(8,128)(2,1)S(1)} %gather_fusion), channel_id=1, source_target_pairs={{0,16},{16,32},{32,48},{48,64},{64,80},{80,96},{96,112},{112,128},... | collective-permute-start | bytes 393224 | tf_op jit(solution)/shard_map/ppermute | solution.py:30
  13.0 8.0 %collective-permute-start.1 = (bf16[4,16,1024]{2,1,0:T(8,128)(2,1)S(1)}, bf16[4,16,1024]{2,1,0:T(8,128)(2,1)S(1)}, u32[]{:S(2)}, u32[]{:S(2)}) collective-permute-start(bf16[4,16,1024]{2,1,0:T(8,128)(2,1)S(1)} %gather_fusion.1), channel_id=1, source_target_pairs={{16,0},{32,16},{48,32},{64,48},{80,64},{96,80},{112,96},{128,112},... | collective-permute-start | bytes 393224 | tf_op jit(solution)/shard_map/ppermute | solution.py:33
  23.6 0.8 copy-start
Sparse Core Ops, SparseCore 0:
  168.3 57.9 reduce-scatter.1

commit v2 on v1

--- a/solution.py
+++ b/solution.py
@@ -14,6 +14,7 @@
 CAP = 24
 NX = 4
 NY = 8
+NZ = 8
 CHUNKS = 7
 
 neg_big = -1e30
@@ -62,12 +63,21 @@
 
 
 def moe_kernel(
-    packed,
+    normed,
+    select,
     mix_hi,
     mix_lo,
+    residual,
     w_in,
     w_out,
     out,
+    tokens,
+    packed,
+    mixed,
+    mixed_send,
+    core_in,
+    z_out,
+    z_in,
     grid_in,
     part,
     relay_in,
@@ -93,6 +103,16 @@
     by_own,
     by_send,
     by_recv,
+    z_own,
+    z_send,
+    z_recv,
+    c_send,
+    c_recv,
+    bc_send,
+    bc_recv,
+    bz_own,
+    bz_send,
+    bz_recv,
 ):
     me = lax.axis_index("req")
     ex = lax.axis_index("exp")
@@ -110,8 +130,19 @@
         yd = lax.rem(y + j, NY)
         return yd, (yd * NX + x, ex)
 
+    z = lax.div(ex, 2)
+    core = lax.rem(ex, 2)
+    other = 1 - core
+    partner = (me, z * 2 + other)
+
+    def zdev(j):
+        zd = lax.rem(z + j, NZ)
+        return zd, (me, zd * 2 + core)
+
     barrier = pltpu.get_barrier_semaphore()
-    for peer in (left, right):
+    for j in range(1, NZ):
+        pl.semaphore_signal(barrier, inc=1, device_id=zdev(j)[1], device_id_type=MESH)
+    for peer in (partner, left, right):
         pl.semaphore_signal(barrier, inc=1, device_id=peer, device_id_type=MESH)
     for j in range(1, NY):
         pl.semaphore_signal(barrier, inc=1, device_id=ydev(j)[1], device_id_type=MESH)
@@ -120,7 +151,7 @@
     load1.start()
     load2.start()
     hidden[...] = jnp.zeros_like(hidden)
-    pl.semaphore_wait(barrier, 2 + NY - 1)
+    pl.semaphore_wait(barrier, 3 + NY - 1 + NZ - 1)
 
     def span(i):
         return pl.ds(pl.multiple_of(i * width, 128), width)
@@ -130,23 +161,15 @@
             src_ref=src, dst_ref=dst, send_sem=send, recv_sem=recv, device_id=dev, device_id_type=MESH
         )
 
-    def issue_y(i, c):
+    def issue_z(i, c):
         cols = span(i)
-        pltpu.make_async_copy(
-            packed.at[lax.div(y, 2), :, cols], grid_in.at[x, y, :, cols], own_sem.at[i]
-        ).start()
-        for j in range(1, NY):
-            yd, dev = ydev(j)
-            remote(
-                packed.at[lax.div(yd, 2), :, cols],
-                grid_in.at[x, y, :, cols],
-                y_send.at[i],
-                y_recv.at[i],
-                dev,
-            ).start()
+        mine = tokens.at[z, core, :, cols]
+        pltpu.make_async_copy(normed.at[:, cols], mine, z_own.at[i]).start()
+        for j in range(1, NZ):
+            remote(normed.at[:, cols], mine, z_send.at[i], z_recv.at[i], zdev(j)[1]).start()
         return c
 
-    lax.fori_loop(0, CHUNKS, issue_y, 0)
+    lax.fori_loop(0, CHUNKS, issue_z, 0)
     load1.wait()
     low, high = pl.ds(0, NY // 2), pl.ds(NY // 2, NY // 2)
 
@@ -157,15 +180,51 @@
         @pl.when(i < CHUNKS)
         def _():
             cols = span(i)
-            wait_bytes(grid_in.at[0, 0, :, cols], own_sem.at[i])
-            wait_bytes(seven(i), y_recv.at[i])
+            wait_bytes(tokens.at[0, 0, :, cols], z_own.at[i])
+            wait_bytes(tokens.at[pl.ds(0, NZ - 1), 0, :, cols], z_recv.at[i])
+            block = tokens.at[:, core, :, cols]
+            remote(block, block, c_send.at[i], c_recv.at[i], partner).start()
+
+        @pl.when((i >= 1) & (i < CHUNKS + 1))
+        def _():
+            n = i - 1
+            cols = span(n)
+            wait_bytes(tokens.at[:, 0, :, cols], c_recv.at[n])
+            packed[:, :, cols] = (
+                jnp.dot(
+                    select[...],
+                    tokens[:, :, :, cols].reshape(select.shape[1], width),
+                    preferred_element_type=jnp.float32,
+                )
+                .astype(jnp.bfloat16)
+                .reshape(EXP_DEV, CAP, width)
+            )
+            pltpu.make_async_copy(
+                packed.at[lax.div(y, 2), :, cols], grid_in.at[x, y, :, cols], own_sem.at[n]
+            ).start()
+            for j in range(1, NY):
+                yd, dev = ydev(j)
+                remote(
+                    packed.at[lax.div(yd, 2), :, cols],
+                    grid_in.at[x, y, :, cols],
+                    y_send.at[n],
+                    y_recv.at[n],
+                    dev,
+                ).start()
+
+        @pl.when((i >= 2) & (i < CHUNKS + 2))
+        def _():
+            n = i - 2
+            cols = span(n)
+            wait_bytes(grid_in.at[0, 0, :, cols], own_sem.at[n])
+            wait_bytes(seven(n), y_recv.at[n])
             block = grid_in.at[x, :, :, cols]
-            remote(block, block, x_send.at[i, 0], x_recv.at[i, 0], right).start()
-            remote(block, block, x_send.at[i, 1], x_recv.at[i, 1], left).start()
-
-        @pl.when((i >= 1) & (i < CHUNKS + 1))
-        def _():
-            n = i - 1
+            remote(block, block, x_send.at[n, 0], x_recv.at[n, 0], right).start()
+            remote(block, block, x_send.at[n, 1], x_recv.at[n, 1], left).start()
+
+        @pl.when((i >= 3) & (i < CHUNKS + 3))
+        def _():
+            n = i - 3
             cols = span(n)
             wait_bytes(grid_in.at[xm, :, :, cols], x_recv.at[n, 0])
             block = grid_in.at[xm, low, :, cols]
@@ -174,9 +233,9 @@
             block = grid_in.at[xp, high, :, cols]
             remote(block, block, r_send.at[n, 1], r_recv.at[n, 1], left).start()
 
-        @pl.when(i >= 2)
-        def _():
-            n = i - 2
+        @pl.when(i >= 4)
+        def _():
+            n = i - 4
             cols = span(n)
             wait_bytes(grid_in.at[xo, low, :, cols], r_recv.at[n, 0])
             wait_bytes(grid_in.at[xo, high, :, cols], r_recv.at[n, 1])
@@ -190,7 +249,7 @@
 
         return c
 
-    lax.fori_loop(0, CHUNKS + 2, inward, 0)
+    lax.fori_loop(0, CHUNKS + 4, inward, 0)
     for b in range(NX):
         v = hidden[b]
         act[b] = (v / (1.0 + jnp.exp(-v))).astype(jnp.bfloat16)
@@ -274,21 +333,53 @@
                     summed.at[yd, :, cols], back.at[y, :, cols], by_send.at[n], by_recv.at[n], dev
                 ).start()
 
-        @pl.when(i >= 3)
+        @pl.when((i >= 3) & (i < CHUNKS + 3))
         def _():
             n = i - 3
             cols = span(n)
             wait_bytes(back.at[0, :, cols], by_own.at[n])
             wait_bytes(back.at[pl.ds(0, NY - 1), :, cols], by_recv.at[n])
             rows = back[:, :, cols].reshape(NY * CAP, width)
-            out[:, cols] = (
-                jnp.dot(mix_hi[...], rows, preferred_element_type=jnp.float32)
-                + jnp.dot(mix_lo[...], rows, preferred_element_type=jnp.float32)
+            total = jnp.dot(mix_hi[...], rows, preferred_element_type=jnp.float32) + jnp.dot(
+                mix_lo[...], rows, preferred_element_type=jnp.float32
+            )
+            total = total.reshape(NZ, 2, -1, width)
+            mixed[:, :, :, cols] = total
+            mixed_send[:, :, :, cols] = total.astype(jnp.bfloat16)
+            remote(
+                mixed_send.at[:, other, :, cols], core_in.at[:, :, cols],
+                bc_send.at[n], bc_recv.at[n], partner,
+            ).start()
+
+        @pl.when((i >= 4) & (i < CHUNKS + 4))
+        def _():
+            n = i - 4
+            cols = span(n)
+            wait_bytes(core_in.at[:, :, cols], bc_recv.at[n])
+            z_out[:, :, cols] = (
+                mixed[:, core, :, cols] + core_in[:, :, cols].astype(jnp.float32)
             ).astype(jnp.bfloat16)
+            pltpu.make_async_copy(z_out.at[z, :, cols], z_in.at[z, :, cols], bz_own.at[n]).start()
+            for j in range(1, NZ):
+                zd, dev = zdev(j)
+                remote(
+                    z_out.at[zd, :, cols], z_in.at[z, :, cols], bz_send.at[n], bz_recv.at[n], dev
+                ).start()
+
+        @pl.when(i >= 5)
+        def _():
+            n = i - 5
+            cols = span(n)
+            wait_bytes(z_in.at[0, :, cols], bz_own.at[n])
+            wait_bytes(z_in.at[pl.ds(0, NZ - 1), :, cols], bz_recv.at[n])
+            total = residual[:, cols]
+            for k in range(NZ):
+                total = total + z_in[k, :, cols].astype(jnp.float32)
+            out[:, cols] = total.astype(jnp.bfloat16)
 
         return c
 
-    lax.fori_loop(0, CHUNKS + 3, outward, 0)
+    lax.fori_loop(0, CHUNKS + 5, outward, 0)
 
     def drain(i, c):
         cols = span(i)
@@ -301,24 +392,36 @@
         for s in range(4):
             wait_bytes(half, bd_send.at[i, s])
         wait_bytes(back.at[pl.ds(0, NY - 1), :, cols], by_send.at[i])
+        wait_bytes(z_in.at[pl.ds(0, NZ - 1), :, cols], z_send.at[i])
+        wait_bytes(z_in.at[:, :, cols], c_send.at[i])
+        wait_bytes(z_in.at[:, :, cols], bc_send.at[i])
+        wait_bytes(z_in.at[pl.ds(0, NZ - 1), :, cols], bz_send.at[i])
         return c
 
     lax.fori_loop(0, CHUNKS, drain, 0)
 
 
-def moe(packed, mix_hi, mix_lo, w_in, w_out):
+def moe(normed, select, mix_hi, mix_lo, residual, w_in, w_out):
     depth, units = w_in.shape
+    rows = normed.shape[0]
     bf = jnp.bfloat16
     vmem = pl.BlockSpec(memory_space=pltpu.VMEM)
     anywhere = pl.BlockSpec(memory_space=pl.ANY)
     dma = pltpu.SemaphoreType.DMA
     return pl.pallas_call(
         moe_kernel,
-        name="moe_plane",
-        out_shape=jax.ShapeDtypeStruct((mix_hi.shape[0], depth), bf),
-        in_specs=[vmem, vmem, vmem, anywhere, anywhere],
+        name="moe_slice",
+        out_shape=jax.ShapeDtypeStruct((rows, depth), bf),
+        in_specs=[vmem, vmem, vmem, vmem, vmem, anywhere, anywhere],
         out_specs=vmem,
         scratch_shapes=[
+            pltpu.VMEM((NZ, 2, rows, depth), bf),
+            pltpu.VMEM((EXP_DEV, CAP, depth), bf),
+            pltpu.VMEM((NZ, 2, rows, depth), jnp.float32),
+            pltpu.VMEM((NZ, 2, rows, depth), bf),
+            pltpu.VMEM((NZ, rows, depth), bf),
+            pltpu.VMEM((NZ, rows, depth), bf),
+            pltpu.VMEM((NZ, rows, depth), bf),
             pltpu.VMEM((NX, NY, CAP, depth), bf),
             pltpu.VMEM((NX, NY, CAP, depth), bf),
             pltpu.VMEM((2, NY // 2, CAP, depth), bf),
@@ -344,11 +447,12 @@
             dma((CHUNKS,)),
             dma((CHUNKS,)),
             dma((CHUNKS,)),
-        ],
+        ]
+        + [dma((CHUNKS,))] * 10,
         compiler_params=pltpu.CompilerParams(
             collective_id=0, has_side_effects=True, vmem_limit_bytes=56 * 1024 * 1024
         ),
-    )(packed, mix_hi, mix_lo, w_in, w_out)
+    )(normed, select, mix_hi, mix_lo, residual, w_in, w_out)
 
 
 def body(
@@ -409,23 +513,15 @@
     gate_local = jnp.sum(jnp.where(matches, gate_values[None, :, :], 0.0), axis=2)
     slot_index = jnp.cumsum(is_named.astype(jnp.int32), axis=1) - 1
     placement = is_named[:, None, :] & (slot_index[:, None, :] == jnp.arange(CAP)[None, :, None])
-    slot_select = placement.astype(jnp.bfloat16)
-    packed = jnp.einsum(
-        "kct,td->kcd",
-        slot_select,
-        lax.all_gather(normed, "exp", axis=0, tiled=True),
-        preferred_element_type=jnp.float32,
-    ).astype(jnp.bfloat16)
+    select = placement.astype(jnp.bfloat16).reshape(EXP_DEV * CAP, -1)
     gated = jnp.where(placement, gate_local[:, None, :], 0.0)
     gated = jnp.broadcast_to(gated[:, None], (EXP_DEV, NY // EXP_DEV) + gated.shape[1:])
     mix = gated.reshape(NY * CAP, -1).T
     mix_hi = lax.reduce_precision(mix, 8, 7)
     mix_lo = (mix - mix_hi).astype(jnp.bfloat16)
-    mixed_rows = moe(packed, mix_hi.astype(jnp.bfloat16), mix_lo, w_in[0, 0], w_out[0, 0])
-    expert_mix = lax.psum_scatter(mixed_rows, "exp", scatter_dimension=0, tiled=True).astype(
-        jnp.float32
-    )
-    return (residual + expert_mix).astype(jnp.bfloat16)
+    return moe(
+        normed, select, mix_hi.astype(jnp.bfloat16), mix_lo, residual, w_in[0, 0], w_out[0, 0]
+    )
 
 
 def solution(mesh):

time: 237 us -> 163 us (0.69)
  waiting for transfers between devices: 58.2 us -> 0.01 us
  blocking collectives: 27.3 us -> 0 us
  Pallas kernels: 115 us -> 142 us
  between operations: 13.7 us -> 0.3 us
    reduce_scatter x1 -> x0, waiting for transfers between devices: 58.1 us -> none  [body(): lax.psum_scatter(mixed_rows, 'exp', scatter_dimension=0, tiled=True)]
    all_gather x1 -> x0, blocking collectives: 27.3 us -> none  [body(): lax.all_gather(normed, 'exp', axis=0, tiled=True)]
    pallas_call x1, Pallas kernels: 115 us -> 142 us  [moe(): pl.pallas_call(moe_kernel, name='moe_slice', out_shape=jax.ShapeDtypeStru...]
  transfers between devices with their start and end apart: 3 -> 2, of which waited for: 2 -> 0; matrix products, arithmetic and copies ran while one was open for 1% -> 2% of each run, Pallas kernels for 0% -> 0%
where the time goes in v2:
time: 163 us
  Pallas kernels  142 us (87%)
  starting transfers between devices  10 us (6%)
  local copies, waits for them, and re-layouts  6.16 us (4%)
  other arithmetic  3.33 us (2%)
    pallas_call x1, Pallas kernels, moe(): pl.pallas_call(moe_kernel, name='moe_slice', out_shape=jax.ShapeDtypeStru...  142 us
    ppermute x1, starting transfers between devices, with_halo(): lax.ppermute(lax.slice_in_dim(block, 0, width, axis=dim), axis, backward)  6.09 us
    ppermute x1, starting transfers between devices, with_halo(): lax.ppermute(lax.slice_in_dim(block, block.shape[dim] - width, None, axis...  3.94 us
  transfers between devices with their start and end apart: 2, of which 0 were waited for; matrix products, arithmetic and copies ran while one was open for 2% of the time, Pallas kernels for 0%

profile of v2, /device:TPU:1, one launch (start us, length us, event | category | flops | bytes accessed | tf_op | source)
XLA Modules:
  0.0 162.7 jit_solution(10726452117870930403)
XLA Ops:
  0.0 1.3 copy.50
  1.4 0.6 gather_fusion
  1.9 3.9 %collective-permute-start = (bf16[4,16,1024]{2,1,0:T(8,128)(2,1)S(1)}, bf16[4,16,1024]{2,1,0:T(8,128)(2,1)S(1)}, u32[]{:S(2)}, u32[]{:S(2)}) collective-permute-start(bf16[4,16,1024]{2,1,0:T(8,128)(2,1)S(1)} %gather_fusion), channel_id=1, source_target_pairs={{0,16},{16,32},{32,48},{48,64},{64,80},{80,96},{96,112},{112,128},... | collective-permute-start | bytes 393224 | tf_op jit(solution)/shard_map/ppermute | solution.py:31
  5.9 0.6 gather_fusion.1
  6.4 6.1 %collective-permute-start.1 = (bf16[4,16,1024]{2,1,0:T(8,128)(2,1)S(1)}, bf16[4,16,1024]{2,1,0:T(8,128)(2,1)S(1)}, u32[]{:S(2)}, u32[]{:S(2)}) collective-permute-start(bf16[4,16,1024]{2,1,0:T(8,128)(2,1)S(1)} %gather_fusion.1), channel_id=1, source_target_pairs={{16,0},{32,16},{48,32},{64,48},{80,64},{96,80},{112,96},{128,112},... | collective-permute-start | bytes 393224 | tf_op jit(solution)/shard_map/ppermute | solution.py:34
  12.8 0.1 compare_reduce_fusion
  12.9 0.3 reduce_window_sum.11
  13.3 0.1 copy.30
  13.4 0.7 fusion.7
  14.2 0.1 reshape.233
  14.4 0.7 fusion.15.select
  15.2 0.8 scatter_fusion
  16.0 0.6 gather_fusion.2
  16.6 0.1 pad_maximum_fusion
  16.7 0.2 reshape.232
  16.9 0.2 reshape.231
  17.1 0.5 fusion.21
  17.6 0.2 fusion.6
  17.8 0.6 fusion.2
  18.5 0.1 copy-done.2
  18.6 0.1 multiply_reduce_fusion
  18.8 0.7 multiply_convert_fusion.normed
  19.5 141.8 %moe_slice.1 = bf16[8,3584]{1,0:T(8,128)(2,1)} custom-call(bf16[8,3584]{1,0:T(8,128)(2,1)} %multiply_convert_fusion.normed, bf16[96,128]{1,0:T(8,128)(2,1)} %fusion.15.select, bf16[128,192]{1,0:T(8,128)(2,1)} %get-tuple-element.10.mix_hi, bf16[128,192]{1,0:T(8,128)(2,1)} %get-tuple-element.9.mix_lo, f32[8,3584]{1,0:T(8,128)} %copy-done, ...), custom_call_target="tpu_custom_call" | custom-call | tf_op jit(solution)/shard_map/moe_slice/pallas_call | solution.py:411
  161.3 1.4 copy.51
  (50 shorter events, 0.6 us)
Async XLA Ops:
  0.0 12.6 %copy-start.7 = (s32[4,8]{1,0:T(4,128)S(1)}, s32[4,8]{1,0:T(4,128)}, u32[]{:S(2)}) copy-start(s32[4,8]{1,0:T(4,128)} %param.17) | copy-start | bytes 388
  0.0 12.7 %copy-start.10 = (s32[4]{0:T(128)S(1)}, s32[4]{0:T(128)}, u32[]{:S(2)}) copy-start(s32[4]{0:T(128)} %param.18) | copy-start | bytes 52
  0.0 1.3 copy-start.8
  0.0 12.6 %copy-start.9 = (s32[1,1,2,4]{3,2,1,0:T(2,128)S(1)}, s32[1,1,2,4]{3,2,1,0:T(2,128)}, u32[]{:S(2)}) copy-start(s32[1,1,2,4]{3,2,1,0:T(2,128)} %param.20) | copy-start | bytes 100
  0.0 12.8 %copy-start.3 = (s32[128,8]{0,1:T(8,128)S(1)}, s32[128,8]{0,1:T(8,128)}, u32[]{:S(2)}) copy-start(s32[128,8]{0,1:T(8,128)} %param.21) | copy-start | bytes 12292
  0.0 13.2 %copy-start.6 = (f32[128,8]{0,1:T(8,128)S(1)}, f32[128,8]{0,1:T(8,128)}, u32[]{:S(2)}) copy-start(f32[128,8]{0,1:T(8,128)} %param.22) | copy-start | bytes 12292
  1.3 12.9 %copy-start.4 = (bf16[8,1024]{1,0:T(8,128)(2,1)S(1)}, bf16[8,1024]{1,0:T(8,128)(2,1)}, u32[]{:S(2)}) copy-start(bf16[8,1024]{1,0:T(8,128)(2,1)} %param.15) | copy-start | bytes 49156
  1.3 12.9 %copy-start.1 = (bf16[8,3584]{1,0:T(8,128)(2,1)S(1)}, bf16[8,3584]{1,0:T(8,128)(2,1)}, u32[]{:S(2)}) copy-start(bf16[8,3584]{1,0:T(8,128)(2,1)} %param.14) | copy-start | bytes 172036
  1.3 13.0 %copy-start.5 = (bf16[3584]{0:T(1024)(128)(2,1)S(1)}, bf16[3584]{0:T(1024)(128)(2,1)}, u32[]{:S(2)}) copy-start(bf16[3584]{0:T(1024)(128)(2,1)} %param.23) | copy-start | bytes 21508
  1.9 13.2 %collective-permute-start = (bf16[4,16,1024]{2,1,0:T(8,128)(2,1)S(1)}, bf16[4,16,1024]{2,1,0:T(8,128)(2,1)S(1)}, u32[]{:S(2)}, u32[]{:S(2)}) collective-permute-start(bf16[4,16,1024]{2,1,0:T(8,128)(2,1)S(1)} %gather_fusion), channel_id=1, source_target_pairs={{0,16},{16,32},{32,48},{48,64},{64,80},{80,96},{96,112},{112,128},... | collective-permute-start | bytes 393224 | tf_op jit(solution)/shard_map/ppermute | solution.py:31
  6.4 8.7 %collective-permute-start.1 = (bf16[4,16,1024]{2,1,0:T(8,128)(2,1)S(1)}, bf16[4,16,1024]{2,1,0:T(8,128)(2,1)S(1)}, u32[]{:S(2)}, u32[]{:S(2)}) collective-permute-start(bf16[4,16,1024]{2,1,0:T(8,128)(2,1)S(1)} %gather_fusion.1), channel_id=1, source_target_pairs={{16,0},{32,16},{48,32},{64,48},{80,64},{96,80},{112,96},{128,112},... | collective-permute-start | bytes 393224 | tf_op jit(solution)/shard_map/ppermute | solution.py:34
  17.8 0.8 copy-start.2
  18.8 0.7 copy-start

commit v3 on v2

v3 whole, which is shorter than its diff:
```python
import functools

import jax
import jax.numpy as jnp
from jax import lax
from jax.experimental import pallas as pl
from jax.experimental.pallas import tpu as pltpu
from jax.sharding import PartitionSpec as P

HEADS = 28
KV_HEADS = 4
HEAD_DIM = 128
EXP_DEV = 4
CAP = 24
TOK = 8
MIGP = 4
NX = 4
NY = 8
NZ = 8
CHUNKS = 14
LAG = 3

neg_big = -1e30
norm_eps = 1e-06
MESH = pl.DeviceIdType.MESH


def wait_bytes(ref, sem):
    pltpu.make_async_copy(ref, ref, sem).wait()


def choose_slots(ex, ids, gates, select, mix_hi, mix_lo):
    count = ids.shape[1]
    earlier = lax.broadcasted_iota(jnp.int32, (count, count), 0)
    later = lax.broadcasted_iota(jnp.int32, (count, count), 1)
    upto = jnp.where(earlier <= later, 1.0, 0.0).astype(jnp.bfloat16)
    slot = lax.broadcasted_iota(jnp.int32, (CAP, count), 0).astype(jnp.float32) + 1.0
    for k in range(EXP_DEV):
        match = ids[...] == ex * EXP_DEV + k
        named = jnp.max(jnp.where(match, 1.0, 0.0), axis=0, keepdims=True)
        gate = jnp.sum(jnp.where(match, gates[...], 0.0), axis=0, keepdims=True)
        row = jnp.broadcast_to(named, (8, count)).astype(jnp.bfloat16)
        order = jnp.dot(row, upto, preferred_element_type=jnp.float32)[:1]
        placed = jnp.where(slot == order, 1.0, 0.0) * named
        select[k] = placed.astype(jnp.bfloat16)
        weight = placed * gate
        upper = weight.astype(jnp.bfloat16)
        lower = (weight - upper.astype(jnp.float32)).astype(jnp.bfloat16)
        for h in range(NY // EXP_DEV):
            mix_hi[k * (NY // EXP_DEV) + h] = upper
            mix_lo[k * (NY // EXP_DEV) + h] = lower


def attend(table, lengths, targets, resid_in, queries, fresh, pool, gain, arriving, cache, residual, normed):
    requests, entries = table.shape
    page = pool.shape[1]
    context = entries * page
    drafts = TOK // requests
    group = HEADS // KV_HEADS

    def gather(i, c):
        entry = table[lax.div(i, entries), lax.rem(i, entries)]
        moved = jnp.int32(0)
        place = jnp.int32(0)
        for side in range(2):
            for p in range(MIGP):
                same = entry == targets[side, p]
                moved = jnp.where(same, 1, moved)
                place = jnp.where(same, side * MIGP + p, place)
        new = arriving[lax.div(place, MIGP), lax.rem(place, MIGP)].astype(jnp.float32)
        old = pool[entry].astype(jnp.float32)
        taken = jnp.broadcast_to(moved, new.shape) > 0
        cache[pl.ds(pl.multiple_of(i * page, page), page), :] = jnp.where(taken, new, old).astype(
            jnp.bfloat16
        )
        return c

    lax.fori_loop(0, requests * entries, gather, 0)
    shape = (group * TOK, requests * context)
    token = lax.rem(lax.broadcasted_iota(jnp.int32, shape, 0), TOK)
    column = lax.broadcasted_iota(jnp.int32, shape, 1)
    holder = lax.div(column, context)
    limit = jnp.zeros(shape, jnp.int32)
    for n in range(requests):
        limit = jnp.where(holder == n, lengths[n], limit)
    cached = (lax.div(token, drafts) == holder) & (lax.rem(column, context) < limit)
    shape = (group * TOK, TOK)
    token = lax.rem(lax.broadcasted_iota(jnp.int32, shape, 0), TOK)
    column = lax.broadcasted_iota(jnp.int32, shape, 1)
    drafted = (lax.div(token, drafts) == lax.div(column, drafts)) & (column <= token)
    values = KV_HEADS * HEAD_DIM
    contract = (((1,), (1,)), ((), ()))

    def weighted(weights, rows):
        upper = weights.astype(jnp.bfloat16)
        lower = (weights - upper.astype(jnp.float32)).astype(jnp.bfloat16)
        return jnp.dot(upper, rows, preferred_element_type=jnp.float32) + jnp.dot(
            lower, rows, preferred_element_type=jnp.float32
        )

    squares = jnp.zeros((TOK, 1), jnp.float32)
    for kv in range(KV_HEADS):
        key_cols = slice(kv * HEAD_DIM, (kv + 1) * HEAD_DIM)
        value_cols = slice(values + kv * HEAD_DIM, values + (kv + 1) * HEAD_DIM)
        heads = [slice(h * HEAD_DIM, (h + 1) * HEAD_DIM) for h in range(kv * group, (kv + 1) * group)]
        query = jnp.concatenate([queries[:, h].astype(jnp.float32) for h in heads], axis=0).astype(
            jnp.bfloat16
        )
        far = lax.dot_general(
            query, cache[:, key_cols], contract, preferred_element_type=jnp.float32
        ) * HEAD_DIM ** (-0.5)
        near = lax.dot_general(
            query, fresh[:, key_cols], contract, preferred_element_type=jnp.float32
        ) * HEAD_DIM ** (-0.5)
        far = jnp.where(cached, far, neg_big)
        near = jnp.where(drafted, near, neg_big)
        highest = jnp.maximum(
            jnp.max(far, axis=1, keepdims=True), jnp.max(near, axis=1, keepdims=True)
        )
        far = jnp.where(cached, jnp.exp(far - highest), 0.0)
        near = jnp.where(drafted, jnp.exp(near - highest), 0.0)
        total = jnp.sum(far, axis=1, keepdims=True) + jnp.sum(near, axis=1, keepdims=True)
        attention = (
            weighted(far, cache[:, value_cols]) + weighted(near, fresh[:, value_cols])
        ) / total
        for g, h in enumerate(heads):
            mine = resid_in[:, h].astype(jnp.float32) + attention[g * TOK : (g + 1) * TOK]
            residual[:, h] = mine
            squares = squares + jnp.sum(mine * mine, axis=1, keepdims=True)
    inverse = lax.rsqrt(squares / (HEADS * HEAD_DIM) + norm_eps)
    normed[...] = (residual[...] * inverse * gain[...].astype(jnp.float32)).astype(jnp.bfloat16)


def layer_kernel(
    table,
    lengths,
    sources,
    targets,
    resid_in,
    queries,
    fresh,
    pool,
    ids,
    gates,
    gain,
    w_in,
    w_out,
    out,
    leaving,
    arriving,
    cache,
    residual,
    normed,
    select,
    mix_hi,
    mix_lo,
    tokens,
    packed,
    mixed,
    mixed_send,
    core_in,
    z_out,
    z_in,
    grid_in,
    part,
    relay_in,
    direct_in,
    summed,
    back,
    w1,
    w2,
    hidden,
    act,
    load_sem,
    page_send,
    page_recv,
    own_sem,
    y_send,
    y_recv,
    x_send,
    x_recv,
    r_send,
    r_recv,
    br_send,
    br_recv,
    bd_send,
    bd_recv,
    by_own,
    by_send,
    by_recv,
    z_own,
    z_send,
    z_recv,
    c_send,
    c_recv,
    bc_send,
    bc_recv,
    bz_own,
    bz_send,
    bz_recv,
):
    me = lax.axis_index("req")
    ex = lax.axis_index("exp")
    x = lax.rem(me, NX)
    y = lax.div(me, NX)
    width = w1.shape[0] // CHUNKS
    row = y * NX
    xp = lax.rem(x + 1, NX)
    xm = lax.rem(x + NX - 1, NX)
    xo = lax.rem(x + 2, NX)
    ring = NX * NY
    after = (lax.rem(me + 1, ring), ex)
    before = (lax.rem(me + ring - 1, ring), ex)
    right = (row + xp, ex)
    left = (row + xm, ex)

    def ydev(j):
        yd = lax.rem(y + j, NY)
        return yd, (yd * NX + x, ex)

    z = lax.div(ex, 2)
    core = lax.rem(ex, 2)
    other = 1 - core
    partner = (me, z * 2 + other)

    def zdev(j):
        zd = lax.rem(z + j, NZ)
        return zd, (me, zd * 2 + core)

    barrier = pltpu.get_barrier_semaphore()
    for j in range(1, NZ):
        pl.semaphore_signal(barrier, inc=1, device_id=zdev(j)[1], device_id_type=MESH)
    for peer in (partner, left, right, after, before):
        pl.semaphore_signal(barrier, inc=1, device_id=peer, device_id_type=MESH)
    for j in range(1, NY):
        pl.semaphore_signal(barrier, inc=1, device_id=ydev(j)[1], device_id_type=MESH)
    load1 = pltpu.make_async_copy(w_in, w1, load_sem.at[0])
    load2 = pltpu.make_async_copy(w_out, w2, load_sem.at[1])
    load1.start()
    load2.start()
    for i in range(MIGP):
        leaving[0, i] = pool[sources[0, i]]
        leaving[1, i] = pool[sources[1, i]]
    hidden[...] = jnp.zeros_like(hidden)
    pl.semaphore_wait(barrier, 5 + NY - 1 + NZ - 1)

    def span(i):
        return pl.ds(pl.multiple_of(i * width, 128), width)

    def remote(src, dst, send, recv, dev):
        return pltpu.make_async_remote_copy(
            src_ref=src, dst_ref=dst, send_sem=send, recv_sem=recv, device_id=dev, device_id_type=MESH
        )

    pages = [
        remote(leaving.at[side], arriving.at[side], page_send.at[side], page_recv.at[side], dev)
        for side, dev in ((0, after), (1, before))
    ]
    for copy in pages:
        copy.start()
    choose_slots(ex, ids, gates, select, mix_hi, mix_lo)
    for copy in pages:
        copy.wait_recv()
    attend(table, lengths, targets, resid_in, queries, fresh, pool, gain, arriving, cache, residual, normed)

    def issue_z(i, c):
        cols = span(i)
        mine = tokens.at[i, z, core]
        pltpu.make_async_copy(normed.at[:, cols], mine, z_own.at[i]).start()
        for j in range(1, NZ):
            remote(normed.at[:, cols], mine, z_send.at[i], z_recv.at[i], zdev(j)[1]).start()
        return c

    lax.fori_loop(0, CHUNKS, issue_z, 0)
    load1.wait()
    low, high = pl.ds(0, NY // 2), pl.ds(NY // 2, NY // 2)

    def seven(i):
        return grid_in.at[i, 0, pl.ds(0, NY - 1)]

    def inward(i, c):
        @pl.when(i < CHUNKS)
        def _():
            cols = span(i)
            wait_bytes(tokens.at[i, 0, 0], z_own.at[i])
            wait_bytes(tokens.at[i, pl.ds(0, NZ - 1), 0], z_recv.at[i])
            block = tokens.at[i, :, core]
            remote(block, block, c_send.at[i], c_recv.at[i], partner).start()

        @pl.when((i >= 1 * LAG) & (i < CHUNKS + 1 * LAG))
        def _():
            n = i - 1 * LAG
            cols = span(n)
            wait_bytes(tokens.at[n, :, 0], c_recv.at[n])
            packed[n] = (
                jnp.dot(
                    select[...].reshape(EXP_DEV * CAP, NZ * 2 * TOK),
                    tokens[n].reshape(NZ * 2 * TOK, width),
                    preferred_element_type=jnp.float32,
                )
                .astype(jnp.bfloat16)
                .reshape(EXP_DEV, CAP, width)
            )
            mine = packed.at[n, lax.div(y, 2)]
            pltpu.make_async_copy(mine, grid_in.at[n, x, 0], own_sem.at[n]).start()
            remote(mine, grid_in.at[n, x, 0], x_send.at[n, 0], x_recv.at[n, 0], right).start()
            remote(mine, grid_in.at[n, x, 0], x_send.at[n, 1], x_recv.at[n, 1], left).start()
            for j in range(1, NY):
                yd, dev = ydev(j)
                remote(
                    packed.at[n, lax.div(yd, 2)],
                    grid_in.at[n, x, NY - j],
                    y_send.at[n],
                    y_recv.at[n],
                    dev,
                ).start()

        @pl.when((i >= 2 * LAG) & (i < CHUNKS + 2 * LAG))
        def _():
            n = i - 2 * LAG
            cols = span(n)
            wait_bytes(seven(n), y_recv.at[n])
            block = grid_in.at[n, x, pl.ds(1, NY - 1)]
            remote(block, block, x_send.at[n, 0], x_recv.at[n, 0], right).start()
            remote(block, block, x_send.at[n, 1], x_recv.at[n, 1], left).start()

        @pl.when((i >= 3 * LAG) & (i < CHUNKS + 3 * LAG))
        def _():
            n = i - 3 * LAG
            cols = span(n)
            wait_bytes(grid_in.at[n, xm], x_recv.at[n, 0])
            block = grid_in.at[n, xm, low]
            remote(block, block, r_send.at[n, 0], r_recv.at[n, 0], right).start()
            wait_bytes(grid_in.at[n, xp], x_recv.at[n, 1])
            block = grid_in.at[n, xp, high]
            remote(block, block, r_send.at[n, 1], r_recv.at[n, 1], left).start()

        @pl.when(i >= 4 * LAG)
        def _():
            n = i - 4 * LAG
            cols = span(n)
            wait_bytes(grid_in.at[n, 0, 0], own_sem.at[n])
            wait_bytes(grid_in.at[n, xo, low], r_recv.at[n, 0])
            wait_bytes(grid_in.at[n, xo, high], r_recv.at[n, 1])
            weight = w1[span(n), :]
            for b in range(NX):
                hidden[b] += jnp.dot(
                    grid_in[n, b].reshape(NY * CAP, width),
                    weight,
                    preferred_element_type=jnp.float32,
                )

        return c

    lax.fori_loop(0, CHUNKS + 4 * LAG, inward, 0)
    for b in range(NX):
        v = hidden[b]
        act[b] = (v / (1.0 + jnp.exp(-v))).astype(jnp.bfloat16)
    load2.wait()

    def outward(i, c):
        @pl.when(i < CHUNKS)
        def _():
            cols = span(i)

            def product(b):
                part[i, b] = (
                    jnp.dot(act[b], w2[:, cols], preferred_element_type=jnp.float32)
                    .astype(jnp.bfloat16)
                    .reshape(NY, CAP, width)
                )

            product(xo)
            product(xm)
            product(xp)
            remote(
                part.at[i, xo, low], relay_in.at[i, 0],
                br_send.at[i, 0], br_recv.at[i, 0], left,
            ).start()
            remote(
                part.at[i, xo, high], relay_in.at[i, 1],
                br_send.at[i, 1], br_recv.at[i, 1], right,
            ).start()
            product(x)
            remote(
                part.at[i, xm, high], direct_in.at[i, 0, high],
                bd_send.at[i, 0], bd_recv.at[i, 0], left,
            ).start()
            remote(
                part.at[i, xp, low], direct_in.at[i, 1, low],
                bd_send.at[i, 1], bd_recv.at[i, 1], right,
            ).start()

        @pl.when((i >= 1 * LAG) & (i < CHUNKS + 1 * LAG))
        def _():
            n = i - 1 * LAG
            cols = span(n)

            def added(b, rows, side):
                wait_bytes(relay_in.at[n, side], br_recv.at[n, side])
                part[n, b, rows] = (
                    part[n, b, rows].astype(jnp.float32)
                    + relay_in[n, side].astype(jnp.float32)
                ).astype(jnp.bfloat16)

            added(xm, low, 0)
            added(xp, high, 1)
            remote(
                part.at[n, xm, low], direct_in.at[n, 0, low],
                bd_send.at[n, 2], bd_recv.at[n, 2], left,
            ).start()
            remote(
                part.at[n, xp, high], direct_in.at[n, 1, high],
                bd_send.at[n, 3], bd_recv.at[n, 3], right,
            ).start()

        @pl.when((i >= 2 * LAG) & (i < CHUNKS + 2 * LAG))
        def _():
            n = i - 2 * LAG
            cols = span(n)
            wait_bytes(direct_in.at[n, 0, high], bd_recv.at[n, 0])
            wait_bytes(direct_in.at[n, 1, low], bd_recv.at[n, 1])
            wait_bytes(direct_in.at[n, 0, low], bd_recv.at[n, 2])
            wait_bytes(direct_in.at[n, 1, high], bd_recv.at[n, 3])
            summed[n] = (
                part[n, x].astype(jnp.float32)
                + direct_in[n, 0].astype(jnp.float32)
                + direct_in[n, 1].astype(jnp.float32)
            ).astype(jnp.bfloat16)
            pltpu.make_async_copy(
                summed.at[n, 0], back.at[n, y], by_own.at[n]
            ).start()
            for j in range(1, NY):
                yd, dev = ydev(j)
                remote(
                    summed.at[n, j], back.at[n, y], by_send.at[n], by_recv.at[n], dev
                ).start()

        @pl.when((i >= 3 * LAG) & (i < CHUNKS + 3 * LAG))
        def _():
            n = i - 3 * LAG
            cols = span(n)
            wait_bytes(back.at[n, 0], by_own.at[n])
            wait_bytes(back.at[n, pl.ds(0, NY - 1)], by_recv.at[n])
            rows = back[n].reshape(NY * CAP, width)
            total = sum(
                lax.dot_general(
                    half[...].reshape(NY * CAP, NZ * 2 * TOK),
                    rows,
                    (((0,), (0,)), ((), ())),
                    preferred_element_type=jnp.float32,
                )
                for half in (mix_hi, mix_lo)
            )
            total = total.reshape(NZ, 2, -1, width)
            mixed[n] = total
            mixed_send[n] = total.astype(jnp.bfloat16)
            remote(
                mixed_send.at[n, :, other], core_in.at[n],
                bc_send.at[n], bc_recv.at[n], partner,
            ).start()

        @pl.when((i >= 4 * LAG) & (i < CHUNKS + 4 * LAG))
        def _():
            n = i - 4 * LAG
            cols = span(n)
            wait_bytes(core_in.at[n], bc_recv.at[n])
            z_out[n] = (
                mixed[n, :, core] + core_in[n].astype(jnp.float32)
            ).astype(jnp.bfloat16)
            pltpu.make_async_copy(z_out.at[n, z], z_in.at[n, z], bz_own.at[n]).start()
            for j in range(1, NZ):
                zd, dev = zdev(j)
                remote(
                    z_out.at[n, zd], z_in.at[n, z], bz_send.at[n], bz_recv.at[n], dev
                ).start()

        @pl.when(i >= 5 * LAG)
        def _():
            n = i - 5 * LAG
            cols = span(n)
            wait_bytes(z_in.at[n, 0], bz_own.at[n])
            wait_bytes(z_in.at[n, pl.ds(0, NZ - 1)], bz_recv.at[n])
            total = residual[:, cols]
            for k in range(NZ):
                total = total + z_in[n, k].astype(jnp.float32)
            out[:, cols] = total.astype(jnp.bfloat16)

        return c

    lax.fori_loop(0, CHUNKS + 5 * LAG, outward, 0)

    def drain(i, c):
        cols = span(i)
        half = relay_in.at[i, 0]
        wait_bytes(seven(i), y_send.at[i])
        for s in range(2):
            wait_bytes(grid_in.at[i, 0], x_send.at[i, s])
            wait_bytes(half, r_send.at[i, s])
            wait_bytes(half, br_send.at[i, s])
        for s in range(4):
            wait_bytes(half, bd_send.at[i, s])
        wait_bytes(back.at[i, pl.ds(0, NY - 1)], by_send.at[i])
        wait_bytes(z_in.at[i, pl.ds(0, NZ - 1)], z_send.at[i])
        wait_bytes(z_in.at[i], c_send.at[i])
        wait_bytes(z_in.at[i], bc_send.at[i])
        wait_bytes(z_in.at[i, pl.ds(0, NZ - 1)], bz_send.at[i])
        return c

    for copy in pages:
        copy.wait_send()
    lax.fori_loop(0, CHUNKS, drain, 0)


def body(
    resid_in,
    queries,
    fresh_kv,
    kv_pool,
    block_table,
    lengths,
    mig_source,
    mig_target,
    expert_ids,
    gate_values,
    norm_gain,
    w_in,
    w_out,
):
    depth, units = w_in.shape[2:]
    rows = resid_in.shape[0]
    pool = kv_pool[0, 0]
    page, wide = pool.shape[1:]
    count = expert_ids.shape[0]
    width = depth // CHUNKS
    bf = jnp.bfloat16
    vmem = pl.BlockSpec(memory_space=pltpu.VMEM)
    smem = pl.BlockSpec(memory_space=pltpu.SMEM)
    anywhere = pl.BlockSpec(memory_space=pl.ANY)
    dma = pltpu.SemaphoreType.DMA
    return pl.pallas_call(
        layer_kernel,
        name="whole_layer",
        out_shape=jax.ShapeDtypeStruct((rows, depth), bf),
        in_specs=[smem] * 4 + [vmem] * 7 + [anywhere] * 2,
        out_specs=vmem,
        scratch_shapes=[
            pltpu.VMEM((2, MIGP, page, wide), bf),
            pltpu.VMEM((2, MIGP, page, wide), bf),
            pltpu.VMEM((block_table.size * page, wide), bf),
            pltpu.VMEM((rows, depth), jnp.float32),
            pltpu.VMEM((rows, depth), bf),
            pltpu.VMEM((EXP_DEV, CAP, count), bf),
            pltpu.VMEM((NY, CAP, count), bf),
            pltpu.VMEM((NY, CAP, count), bf),
            pltpu.VMEM((CHUNKS, NZ, 2, rows, width), bf),
            pltpu.VMEM((CHUNKS, EXP_DEV, CAP, width), bf),
            pltpu.VMEM((CHUNKS, NZ, 2, rows, width), jnp.float32),
            pltpu.VMEM((CHUNKS, NZ, 2, rows, width), bf),
            pltpu.VMEM((CHUNKS, NZ, rows, width), bf),
            pltpu.VMEM((CHUNKS, NZ, rows, width), bf),
            pltpu.VMEM((CHUNKS, NZ, rows, width), bf),
            pltpu.VMEM((CHUNKS, NX, NY, CAP, width), bf),
            pltpu.VMEM((CHUNKS, NX, NY, CAP, width), bf),
            pltpu.VMEM((CHUNKS, 2, NY // 2, CAP, width), bf),
            pltpu.VMEM((CHUNKS, 2, NY, CAP, width), bf),
            pltpu.VMEM((CHUNKS, NY, CAP, width), bf),
            pltpu.VMEM((CHUNKS, NY, CAP, width), bf),
            pltpu.VMEM((depth, units), bf),
            pltpu.VMEM((units, depth), bf),
            pltpu.VMEM((NX, NY * CAP, units), jnp.float32),
            pltpu.VMEM((NX, NY * CAP, units), bf),
            dma((2,)),
            dma((2,)),
            dma((2,)),
            dma((CHUNKS,)),
            dma((CHUNKS,)),
            dma((CHUNKS,)),
            dma((CHUNKS, 2)),
            dma((CHUNKS, 2)),
            dma((CHUNKS, 2)),
            dma((CHUNKS, 2)),
            dma((CHUNKS, 2)),
            dma((CHUNKS, 2)),
            dma((CHUNKS, 4)),
            dma((CHUNKS, 4)),
            dma((CHUNKS,)),
            dma((CHUNKS,)),
            dma((CHUNKS,)),
        ]
        + [dma((CHUNKS,))] * 10,
        compiler_params=pltpu.CompilerParams(
            collective_id=0, has_side_effects=True, vmem_limit_bytes=56 * 1024 * 1024
        ),
    )(
        block_table,
        lengths,
        mig_source[0, 0],
        mig_target[0, 0],
        resid_in,
        queries,
        fresh_kv,
        pool,
        expert_ids.T,
        gate_values.T,
        norm_gain[None],
        w_in[0, 0],
        w_out[0, 0],
    )


def solution(mesh):
    placed = (
        P(("req", "exp"), None),
        P(("req", "exp"), None),
        P(("req", "exp"), None),
        P("req", "exp", None, None, None),
        P(("req", "exp"), None),
        P(("req", "exp")),
        P("req", "exp", None, None),
        P("req", "exp", None, None),
        P("req", None),
        P("req", None),
        P(),
        P("exp", "req", None, None),
        P("exp", "req", None, None),
    )
    return jax.shard_map(
        body, mesh=mesh, in_specs=placed, out_specs=P(("req", "exp"), None), check_vma=False
    )
```

time: 163 us -> 150 us (0.920)
  starting transfers between devices: 10 us -> 0 us
  Pallas kernels: 142 us -> 146 us
  local copies, waits for them, and re-layouts: 6.16 us -> 2.75 us
  other arithmetic: 3.33 us -> 0 us
    ppermute x2 -> x0, starting transfers between devices: 10 us -> none  [the longest x1 6.09 us: with_halo(): lax.ppermute(lax.slice_in_dim(block, 0, width, axis=dim), axis, backward)]
    pallas_call x1, Pallas kernels: 142 us -> 146 us  [body(): pl.pallas_call(layer_kernel, name='whole_layer', out_shape=jax.ShapeDtype...]
    convert_element_type x5 -> x0, other arithmetic: 2.11 us -> none  [the longest x1 0.71 us: body(): (residual * inv_rms * norm_gain.astype(jnp.float32)).astype(jnp.bfloat16)]
    gather x3 -> x0, local copies, waits for them, and re-layouts: 1.72 us -> none  [the longest x1 0.61 us: body(): pool_after[block_table].reshape(request_count, cache_span, kv_width)]
  transfers between devices with their start and end apart: 2 -> 0, of which waited for: 0 -> 0; matrix products, arithmetic and copies ran while one was open for 2% -> 0% of each run, Pallas kernels for 0% -> 0%
where the time goes in v3:
time: 150 us; the launch traced here: 149 us
  Pallas kernels  146 us (97%)
  local copies, waits for them, and re-layouts  2.75 us (2%)
    pallas_call x1, Pallas kernels, body(): pl.pallas_call(layer_kernel, name='whole_layer', out_shape=jax.ShapeDtype...  146 us

profile of v3, /device:TPU:1, one launch (start us, length us, event | category | flops | bytes accessed | tf_op | source)
XLA Modules:
  0.0 149.2 jit_solution(1058978762433683205)
XLA Ops:
  0.0 1.3 broadcast_in_dim.3.gain
  1.3 146.4 %whole_layer.1 = bf16[8,3584]{1,0:T(8,128)(2,1)} custom-call(s32[4,8]{1,0:T(4,128)} %table.1, s32[4]{0:T(128)} %lengths.1, s32[2,4]{1,0:T(2,128)} %bitcast.12, s32[2,4]{1,0:T(2,128)} %bitcast.13, bf16[8,3584]{1,0:T(8,128)(2,1)} %resid_in.1, bf16[8,3584]{1,0:T(8,128)(2,1)} %queries.1, bf16[8,1024]{1,0:T(8,128)(2,1)} %fresh.1, bf16[32,16,1024]{2,1,0:T(8,128)(2,1)} %bitcast.9, ...), custom_call_target="tpu_custom_call" | custom-call | tf_op jit(solution)/shard_map/whole_layer/pallas_call | solution.py:541
  147.7 1.4 copy.15

commit v4 on v3

--- a/solution.py
+++ b/solution.py
@@ -18,7 +18,9 @@
 NY = 8
 NZ = 8
 CHUNKS = 14
-LAG = 3
+SHARED = 9
+INWARD = (0, 1, 3, 5, 9, 7)
+OUTWARD = (0, 4, 6, 8, 9, 11, 2)
 
 neg_big = -1e30
 norm_eps = 1e-06
@@ -51,6 +53,20 @@
             mix_lo[k * (NY // EXP_DEV) + h] = lower
 
 
+def stay_pages(table, pool, cache):
+    requests, entries = table.shape
+    page = pool.shape[1]
+    rest = entries - MIGP
+
+    def copy(i, c):
+        n, p = lax.div(i, rest), MIGP + lax.rem(i, rest)
+        start = pl.multiple_of((n * entries + p) * page, page)
+        cache[pl.ds(start, page), :] = pool[table[n, p]]
+        return c
+
+    lax.fori_loop(0, requests * rest, copy, 0)
+
+
 def attend(table, lengths, targets, resid_in, queries, fresh, pool, gain, arriving, cache, residual, normed):
     requests, entries = table.shape
     page = pool.shape[1]
@@ -59,23 +75,18 @@
     group = HEADS // KV_HEADS
 
     def gather(i, c):
-        entry = table[lax.div(i, entries), lax.rem(i, entries)]
-        moved = jnp.int32(0)
-        place = jnp.int32(0)
+        n, p = lax.div(i, MIGP), lax.rem(i, MIGP)
+        entry = table[n, p]
+        old = pool[entry].astype(jnp.float32)
         for side in range(2):
-            for p in range(MIGP):
-                same = entry == targets[side, p]
-                moved = jnp.where(same, 1, moved)
-                place = jnp.where(same, side * MIGP + p, place)
-        new = arriving[lax.div(place, MIGP), lax.rem(place, MIGP)].astype(jnp.float32)
-        old = pool[entry].astype(jnp.float32)
-        taken = jnp.broadcast_to(moved, new.shape) > 0
-        cache[pl.ds(pl.multiple_of(i * page, page), page), :] = jnp.where(taken, new, old).astype(
-            jnp.bfloat16
-        )
+            moved = jnp.where(entry == targets[side, p], 1, 0)
+            new = arriving[side, p].astype(jnp.float32)
+            old = jnp.where(jnp.broadcast_to(moved, new.shape) > 0, new, old)
+        start = pl.multiple_of((n * entries + p) * page, page)
+        cache[pl.ds(start, page), :] = old.astype(jnp.bfloat16)
         return c
 
-    lax.fori_loop(0, requests * entries, gather, 0)
+    lax.fori_loop(0, requests * MIGP, gather, 0)
     shape = (group * TOK, requests * context)
     token = lax.rem(lax.broadcasted_iota(jnp.int32, shape, 0), TOK)
     column = lax.broadcasted_iota(jnp.int32, shape, 1)
@@ -164,6 +175,7 @@
     grid_in,
     part,
     relay_in,
+    pair_in,
     direct_in,
     summed,
     back,
@@ -198,6 +210,10 @@
     bz_own,
     bz_send,
     bz_recv,
+    p_send,
+    p_recv,
+    bp_send,
+    bp_recv,
 ):
     me = lax.axis_index("req")
     ex = lax.axis_index("exp")
@@ -259,6 +275,7 @@
     for copy in pages:
         copy.start()
     choose_slots(ex, ids, gates, select, mix_hi, mix_lo)
+    stay_pages(table, pool, cache)
     for copy in pages:
         copy.wait_recv()
     attend(table, lengths, targets, resid_in, queries, fresh, pool, gain, arriving, cache, residual, normed)
@@ -274,6 +291,10 @@
     lax.fori_loop(0, CHUNKS, issue_z, 0)
     load1.wait()
     low, high = pl.ds(0, NY // 2), pl.ds(NY // 2, NY // 2)
+    odd = lax.rem(y, 2)
+    twin = ((y + 1 - 2 * odd) * NX + x, ex)
+    low_mine, high_mine = pl.ds(2 * odd, 2), pl.ds(NY // 2 + 2 * odd, 2)
+    low_twin, high_twin = pl.ds(2 - 2 * odd, 2), pl.ds(NY // 2 + 2 - 2 * odd, 2)
 
     def seven(i):
         return grid_in.at[i, 0, pl.ds(0, NY - 1)]
@@ -287,9 +308,9 @@
             block = tokens.at[i, :, core]
             remote(block, block, c_send.at[i], c_recv.at[i], partner).start()
 
-        @pl.when((i >= 1 * LAG) & (i < CHUNKS + 1 * LAG))
-        def _():
-            n = i - 1 * LAG
+        @pl.when((i >= INWARD[1]) & (i < CHUNKS + INWARD[1]))
+        def _():
+            n = i - INWARD[1]
             cols = span(n)
             wait_bytes(tokens.at[n, :, 0], c_recv.at[n])
             packed[n] = (
@@ -302,46 +323,74 @@
                 .reshape(EXP_DEV, CAP, width)
             )
             mine = packed.at[n, lax.div(y, 2)]
-            pltpu.make_async_copy(mine, grid_in.at[n, x, 0], own_sem.at[n]).start()
-            remote(mine, grid_in.at[n, x, 0], x_send.at[n, 0], x_recv.at[n, 0], right).start()
-            remote(mine, grid_in.at[n, x, 0], x_send.at[n, 1], x_recv.at[n, 1], left).start()
+            spot = grid_in.at[n, x, y]
+            pltpu.make_async_copy(mine, spot, own_sem.at[n]).start()
+            remote(mine, spot, x_send.at[n, 0], x_recv.at[n, 0], right).start()
+            remote(mine, spot, x_send.at[n, 1], x_recv.at[n, 1], left).start()
             for j in range(1, NY):
                 yd, dev = ydev(j)
                 remote(
                     packed.at[n, lax.div(yd, 2)],
-                    grid_in.at[n, x, NY - j],
+                    spot,
                     y_send.at[n],
                     y_recv.at[n],
                     dev,
                 ).start()
 
-        @pl.when((i >= 2 * LAG) & (i < CHUNKS + 2 * LAG))
-        def _():
-            n = i - 2 * LAG
+        @pl.when((i >= INWARD[2]) & (i < CHUNKS + INWARD[2]))
+        def _():
+            n = i - INWARD[2]
             cols = span(n)
             wait_bytes(seven(n), y_recv.at[n])
-            block = grid_in.at[n, x, pl.ds(1, NY - 1)]
-            remote(block, block, x_send.at[n, 0], x_recv.at[n, 0], right).start()
-            remote(block, block, x_send.at[n, 1], x_recv.at[n, 1], left).start()
-
-        @pl.when((i >= 3 * LAG) & (i < CHUNKS + 3 * LAG))
-        def _():
-            n = i - 3 * LAG
+            for j in range(1, NY):
+                block = grid_in.at[n, x, lax.rem(y + j, NY)]
+                remote(block, block, x_send.at[n, 0], x_recv.at[n, 0], right).start()
+                remote(block, block, x_send.at[n, 1], x_recv.at[n, 1], left).start()
+
+        @pl.when((i >= INWARD[3]) & (i < CHUNKS + INWARD[3]))
+        def _():
+            n = i - INWARD[3]
             cols = span(n)
             wait_bytes(grid_in.at[n, xm], x_recv.at[n, 0])
-            block = grid_in.at[n, xm, low]
-            remote(block, block, r_send.at[n, 0], r_recv.at[n, 0], right).start()
             wait_bytes(grid_in.at[n, xp], x_recv.at[n, 1])
-            block = grid_in.at[n, xp, high]
-            remote(block, block, r_send.at[n, 1], r_recv.at[n, 1], left).start()
-
-        @pl.when(i >= 4 * LAG)
-        def _():
-            n = i - 4 * LAG
+
+            def pass_on(first, second):
+                block = grid_in.at[n, xm, first]
+                remote(block, block, r_send.at[n, 0], r_recv.at[n, 0], right).start()
+                block = grid_in.at[n, xp, second]
+                remote(block, block, r_send.at[n, 1], r_recv.at[n, 1], left).start()
+
+            @pl.when(n < SHARED)
+            def _():
+                pass_on(low_mine, high_mine)
+
+            @pl.when(n >= SHARED)
+            def _():
+                pass_on(low, high)
+
+        @pl.when((i >= INWARD[5]) & (i < SHARED + INWARD[5]))
+        def _():
+            n = i - INWARD[5]
+            for side, rows in ((0, low_mine), (1, high_mine)):
+                block = grid_in.at[n, xo, rows]
+                wait_bytes(block, r_recv.at[n, side])
+                remote(block, block, p_send.at[n], p_recv.at[n], twin).start()
+
+        @pl.when(i >= INWARD[4])
+        def _():
+            n = i - INWARD[4]
             cols = span(n)
             wait_bytes(grid_in.at[n, 0, 0], own_sem.at[n])
-            wait_bytes(grid_in.at[n, xo, low], r_recv.at[n, 0])
-            wait_bytes(grid_in.at[n, xo, high], r_recv.at[n, 1])
+
+            @pl.when(n < SHARED)
+            def _():
+                wait_bytes(grid_in.at[n, xo, low], p_recv.at[n])
+
+            @pl.when(n >= SHARED)
+            def _():
+                wait_bytes(grid_in.at[n, xo, low], r_recv.at[n, 0])
+                wait_bytes(grid_in.at[n, xo, high], r_recv.at[n, 1])
+
             weight = w1[span(n), :]
             for b in range(NX):
                 hidden[b] += jnp.dot(
@@ -352,7 +401,7 @@
 
         return c
 
-    lax.fori_loop(0, CHUNKS + 4 * LAG, inward, 0)
+    lax.fori_loop(0, CHUNKS + INWARD[4], inward, 0)
     for b in range(NX):
         v = hidden[b]
         act[b] = (v / (1.0 + jnp.exp(-v))).astype(jnp.bfloat16)
@@ -371,17 +420,25 @@
                 )
 
             product(xo)
+
+            @pl.when(i < SHARED)
+            def _():
+                for side, rows in ((0, low_twin), (1, high_twin)):
+                    remote(
+                        part.at[i, xo, rows], pair_in.at[i, side], bp_send.at[i], bp_recv.at[i], twin
+                    ).start()
+
+            @pl.when(i >= SHARED)
+            def _():
+                remote(
+                    part.at[i, xo, low], relay_in.at[i, 0], br_send.at[i, 0], br_recv.at[i, 0], left
+                ).start()
+                remote(
+                    part.at[i, xo, high], relay_in.at[i, 1], br_send.at[i, 1], br_recv.at[i, 1], right
+                ).start()
+
             product(xm)
             product(xp)
-            remote(
-                part.at[i, xo, low], relay_in.at[i, 0],
-                br_send.at[i, 0], br_recv.at[i, 0], left,
-            ).start()
-            remote(
-                part.at[i, xo, high], relay_in.at[i, 1],
-                br_send.at[i, 1], br_recv.at[i, 1], right,
-            ).start()
-            product(x)
             remote(
                 part.at[i, xm, high], direct_in.at[i, 0, high],
                 bd_send.at[i, 0], bd_recv.at[i, 0], left,
@@ -390,21 +447,42 @@
                 part.at[i, xp, low], direct_in.at[i, 1, low],
                 bd_send.at[i, 1], bd_recv.at[i, 1], right,
             ).start()
-
-        @pl.when((i >= 1 * LAG) & (i < CHUNKS + 1 * LAG))
-        def _():
-            n = i - 1 * LAG
-            cols = span(n)
-
-            def added(b, rows, side):
-                wait_bytes(relay_in.at[n, side], br_recv.at[n, side])
+            product(x)
+
+        @pl.when((i >= OUTWARD[6]) & (i < SHARED + OUTWARD[6]))
+        def _():
+            n = i - OUTWARD[6]
+            wait_bytes(pair_in.at[n], bp_recv.at[n])
+            for side, rows, dev in ((0, low_mine, left), (1, high_mine, right)):
+                part[n, xo, rows] = (
+                    part[n, xo, rows].astype(jnp.float32) + pair_in[n, side].astype(jnp.float32)
+                ).astype(jnp.bfloat16)
+                remote(
+                    part.at[n, xo, rows], relay_in.at[n, side, low_mine],
+                    br_send.at[n, side], br_recv.at[n, side], dev,
+                ).start()
+
+        @pl.when((i >= OUTWARD[1]) & (i < CHUNKS + OUTWARD[1]))
+        def _():
+            n = i - OUTWARD[1]
+
+            def added(b, rows, side, inner):
+                wait_bytes(relay_in.at[n, side, inner], br_recv.at[n, side])
                 part[n, b, rows] = (
                     part[n, b, rows].astype(jnp.float32)
-                    + relay_in[n, side].astype(jnp.float32)
+                    + relay_in[n, side, inner].astype(jnp.float32)
                 ).astype(jnp.bfloat16)
 
-            added(xm, low, 0)
-            added(xp, high, 1)
+            @pl.when(n < SHARED)
+            def _():
+                added(xm, low_mine, 0, low_mine)
+                added(xp, high_mine, 1, low_mine)
+
+            @pl.when(n >= SHARED)
+            def _():
+                added(xm, low, 0, low)
+                added(xp, high, 1, low)
+
             remote(
                 part.at[n, xm, low], direct_in.at[n, 0, low],
                 bd_send.at[n, 2], bd_recv.at[n, 2], left,
@@ -414,9 +492,9 @@
                 bd_send.at[n, 3], bd_recv.at[n, 3], right,
             ).start()
 
-        @pl.when((i >= 2 * LAG) & (i < CHUNKS + 2 * LAG))
-        def _():
-            n = i - 2 * LAG
+        @pl.when((i >= OUTWARD[2]) & (i < CHUNKS + OUTWARD[2]))
+        def _():
+            n = i - OUTWARD[2]
             cols = span(n)
             wait_bytes(direct_in.at[n, 0, high], bd_recv.at[n, 0])
             wait_bytes(direct_in.at[n, 1, low], bd_recv.at[n, 1])
@@ -428,17 +506,17 @@
                 + direct_in[n, 1].astype(jnp.float32)
             ).astype(jnp.bfloat16)
             pltpu.make_async_copy(
-                summed.at[n, 0], back.at[n, y], by_own.at[n]
+                summed.at[n, y], back.at[n, y], by_own.at[n]
             ).start()
             for j in range(1, NY):
                 yd, dev = ydev(j)
                 remote(
-                    summed.at[n, j], back.at[n, y], by_send.at[n], by_recv.at[n], dev
+                    summed.at[n, yd], back.at[n, y], by_send.at[n], by_recv.at[n], dev
                 ).start()
 
-        @pl.when((i >= 3 * LAG) & (i < CHUNKS + 3 * LAG))
-        def _():
-            n = i - 3 * LAG
+        @pl.when((i >= OUTWARD[3]) & (i < CHUNKS + OUTWARD[3]))
+        def _():
+            n = i - OUTWARD[3]
             cols = span(n)
             wait_bytes(back.at[n, 0], by_own.at[n])
             wait_bytes(back.at[n, pl.ds(0, NY - 1)], by_recv.at[n])
@@ -460,9 +538,9 @@
                 bc_send.at[n], bc_recv.at[n], partner,
             ).start()
 
-        @pl.when((i >= 4 * LAG) & (i < CHUNKS + 4 * LAG))
-        def _():
-            n = i - 4 * LAG
+        @pl.when((i >= OUTWARD[4]) & (i < CHUNKS + OUTWARD[4]))
+        def _():
+            n = i - OUTWARD[4]
             cols = span(n)
             wait_bytes(core_in.at[n], bc_recv.at[n])
             z_out[n] = (
@@ -475,9 +553,9 @@
                     z_out.at[n, zd], z_in.at[n, z], bz_send.at[n], bz_recv.at[n], dev
                 ).start()
 
-        @pl.when(i >= 5 * LAG)
-        def _():
-            n = i - 5 * LAG
+        @pl.when(i >= OUTWARD[5])
+        def _():
+            n = i - OUTWARD[5]
             cols = span(n)
             wait_bytes(z_in.at[n, 0], bz_own.at[n])
             wait_bytes(z_in.at[n, pl.ds(0, NZ - 1)], bz_recv.at[n])
@@ -488,7 +566,7 @@
 
         return c
 
-    lax.fori_loop(0, CHUNKS + 5 * LAG, outward, 0)
+    lax.fori_loop(0, CHUNKS + OUTWARD[5], outward, 0)
 
     def drain(i, c):
         cols = span(i)
@@ -496,11 +574,24 @@
         wait_bytes(seven(i), y_send.at[i])
         for s in range(2):
             wait_bytes(grid_in.at[i, 0], x_send.at[i, s])
-            wait_bytes(half, r_send.at[i, s])
-            wait_bytes(half, br_send.at[i, s])
         for s in range(4):
             wait_bytes(half, bd_send.at[i, s])
         wait_bytes(back.at[i, pl.ds(0, NY - 1)], by_send.at[i])
+
+        @pl.when(i < SHARED)
+        def _():
+            for s in range(2):
+                wait_bytes(pair_in.at[i, 0], r_send.at[i, s])
+                wait_bytes(pair_in.at[i, 0], br_send.at[i, s])
+            wait_bytes(pair_in.at[i], p_send.at[i])
+            wait_bytes(pair_in.at[i], bp_send.at[i])
+
+        @pl.when(i >= SHARED)
+        def _():
+            for s in range(2):
+                wait_bytes(half, r_send.at[i, s])
+                wait_bytes(half, br_send.at[i, s])
+
         wait_bytes(z_in.at[i, pl.ds(0, NZ - 1)], z_send.at[i])
         wait_bytes(z_in.at[i], c_send.at[i])
         wait_bytes(z_in.at[i], bc_send.at[i])
@@ -563,6 +654,7 @@
             pltpu.VMEM((CHUNKS, NX, NY, CAP, width), bf),
             pltpu.VMEM((CHUNKS, NX, NY, CAP, width), bf),
             pltpu.VMEM((CHUNKS, 2, NY // 2, CAP, width), bf),
+            pltpu.VMEM((CHUNKS, 2, 2, CAP, width), bf),
             pltpu.VMEM((CHUNKS, 2, NY, CAP, width), bf),
             pltpu.VMEM((CHUNKS, NY, CAP, width), bf),
             pltpu.VMEM((CHUNKS, NY, CAP, width), bf),
@@ -588,7 +680,7 @@
             dma((CHUNKS,)),
             dma((CHUNKS,)),
         ]
-        + [dma((CHUNKS,))] * 10,
+        + [dma((CHUNKS,))] * 14,
         compiler_params=pltpu.CompilerParams(
             collective_id=0, has_side_effects=True, vmem_limit_bytes=56 * 1024 * 1024
         ),

time: 150 us -> 146 us (0.973)
  Pallas kernels: 146 us -> 143 us
    pallas_call x1, Pallas kernels: 146 us -> 143 us  [body(): pl.pallas_call(layer_kernel, name='whole_layer', out_shape=jax.ShapeDtype...]
where the time goes in v4:
time: 146 us; the launch traced here: 145 us
  Pallas kernels  143 us (98%)
  local copies, waits for them, and re-layouts  2.75 us (2%)
    pallas_call x1, Pallas kernels, body(): pl.pallas_call(layer_kernel, name='whole_layer', out_shape=jax.ShapeDtype...  143 us

profile of v4, /device:TPU:1, one launch (start us, length us, event | category | flops | bytes accessed | tf_op | source)
XLA Modules:
  0.0 145.4 jit_solution(2187653125176176121)
XLA Ops:
  0.0 1.3 broadcast_in_dim.3.gain
  1.3 142.7 %whole_layer.1 = bf16[8,3584]{1,0:T(8,128)(2,1)} custom-call(s32[4,8]{1,0:T(4,128)} %table.1, s32[4]{0:T(128)} %lengths.1, s32[2,4]{1,0:T(2,128)} %bitcast.12, s32[2,4]{1,0:T(2,128)} %bitcast.13, bf16[8,3584]{1,0:T(8,128)(2,1)} %resid_in.1, bf16[8,3584]{1,0:T(8,128)(2,1)} %queries.1, bf16[8,1024]{1,0:T(8,128)(2,1)} %fresh.1, bf16[32,16,1024]{2,1,0:T(8,128)(2,1)} %bitcast.9, ...), custom_call_target="tpu_custom_call" | custom-call | tf_op jit(solution)/shard_map/whole_layer/pallas_call | solution.py:632
  144.0 1.4 copy.15
